TPU v7x, 32 devices: a whole 2x2x4 slice. The times are simulated.
32 devices in a mesh: groups: 2 (over x), rows: 8 (over z, y), cols: 2 (over core).
Axes of the slice: x: 2, y: 2, z: 4, core: 2. Of those that a mesh axis runs over, the one named last changes fastest.
Arguments:
- depth: float32 [4096, 512], P(('groups', 'rows'), 'cols'), parts along dimension 0, may hold values from 0 to 1.5, as said below
- velocity: float32 [2, 4096, 512], P(None, ('groups', 'rows'), 'cols'), parts along dimension 1, may hold values from -1 to 1
- bed: float32 [4096, 512], P(('groups', 'rows'), 'cols'), parts along dimension 0, may hold values from 0 to 0.5
- slots: int32 [16, 2, 3], P(('groups', 'rows'), 'cols'), parts along dimension 0, may hold values from -1 to 63, as said below
Outputs:
- packed: float32 [16, 2, 3, 3, 128, 128], P(('groups', 'rows'), 'cols'), parts along dimension 0
There are 2 independent parts, one for each index of `groups`. A program takes and returns all parts, laid end to end along the dimension named above; each array names one. Nothing has to cross between parts.
Inputs may be any that keep to these rules, and one draw needn't show every extreme that they name: Each non-negative entry of slots[r, c] is the id of a tile of device (r, c)'s own block (tile rows r * 2 to r * 2 + 1, tile columns c * 2 to c * 2 + 1) or of the block of its partner, device ((r + 4) mod 8, c). No id is listed twice. Every device's partner lists at least one and at most 2 tiles of that device's block, and some device's partner lists exactly 2; at most 3 entries of one list are ids, and some list has exactly 3. `depth`: depth is zero on every cell of a tile that no slot list names.
All inputs are finite; a program needn't handle non-finite values.
Results may differ from a plain program's by a relative error of at most 0.0003.
Values sent between devices are 32-bit elements; how exact they have to be, the bound alone decides.
No kernel may reach another device: no remote copies, remote signals or barrier semaphores. Data moves between devices by JAX's collectives and lax.ppermute only.
A program may use at most 64 MiB of HBM per device.

v0:
```python
import jax
import jax.numpy as jnp
from jax import lax
from jax.sharding import PartitionSpec as P

TILE = 128
RT = 2
CT = 2


GRAVITY = 9.81
TIME_STEP = 0.04
DRY_DEPTH = 0.05
SPEED_FLOOR = 0.5


def passed_along(block, axis, distance):
    devices = range(lax.axis_size(axis))
    route = [((i - distance) % len(devices), i) for i in devices]
    return lax.ppermute(block, axis, route)


def with_halo(cells, sides, width):
    for axis, dim in sides:
        count = lax.axis_size(axis)
        ends = count - 1
        head = lax.slice_in_dim(cells, 0, width, axis=dim)
        tail = lax.slice_in_dim(cells, cells.shape[dim] - width, cells.shape[dim], axis=dim)
        cells = jnp.concatenate(
            [
                lax.ppermute(tail, axis, [(i, (i + 1) % count) for i in range(ends)]),
                cells,
                lax.ppermute(head, axis, [((i + 1) % count, i) for i in range(ends)]),
            ],
            axis=dim,
        )
    return cells


def take_range(values, lower_end, upper_end, direction):
    selector = [slice(None)] * values.ndim
    selector[direction] = slice(lower_end, upper_end)
    return values[tuple(selector)]


def minmod(left_diff, right_diff):
    return (
        0.5
        * (jnp.sign(left_diff) + jnp.sign(right_diff))
        * jnp.minimum(jnp.abs(left_diff), jnp.abs(right_diff))
    )


def face_values(values, direction):
    change = take_range(values, 1, None, direction) - take_range(values, 0, -1, direction)
    slope = minmod(take_range(change, 0, -1, direction), take_range(change, 1, None, direction))
    middle = take_range(values, 1, -1, direction)
    return (middle - 0.5 * slope, middle + 0.5 * slope)


def velocity_from(water, flow):
    return 2.0 * water * flow / (water * water + jnp.maximum(water * water, DRY_DEPTH * DRY_DEPTH))


def flux_sweep(water, normal, across, ground, direction):
    water_low, water_high = face_values(water, direction)
    normal_low, normal_high = face_values(normal, direction)
    across_low, across_high = face_values(across, direction)
    ground_low, ground_high = face_values(ground, direction)

    def left_side(values):
        return take_range(values, 0, -1, direction)

    def right_side(values):
        return take_range(values, 1, None, direction)

    water_left = left_side(water_high)
    water_right = right_side(water_low)
    speed_left = velocity_from(water_left, left_side(normal_high))
    speed_right = velocity_from(water_right, right_side(normal_low))
    drift_left = velocity_from(water_left, left_side(across_high))
    drift_right = velocity_from(water_right, right_side(across_low))
    ground_left = left_side(ground_high)
    ground_right = right_side(ground_low)
    ground_top = jnp.maximum(ground_left, ground_right)
    level_left = jnp.maximum(0.0, water_left + ground_left - ground_top)
    level_right = jnp.maximum(0.0, water_right + ground_right - ground_top)
    wave_left = jnp.sqrt(GRAVITY * level_left)
    wave_right = jnp.sqrt(GRAVITY * level_right)
    lower_speed = jnp.minimum(jnp.minimum(speed_left - wave_left, speed_right - wave_right), 0.0)
    upper_speed = jnp.maximum(jnp.maximum(speed_left + wave_left, speed_right + wave_right), 0.0)
    spread = jnp.maximum(upper_speed - lower_speed, SPEED_FLOOR)

    def riemann_flux(flux_left, flux_right, kept_left, kept_right):
        return (
            upper_speed * flux_left
            - lower_speed * flux_right
            + upper_speed * lower_speed * (kept_right - kept_left)
        ) / spread

    mass_left = level_left * speed_left
    mass_right = level_right * speed_right
    mass_flux = riemann_flux(mass_left, mass_right, level_left, level_right)
    push_flux = riemann_flux(
        mass_left * speed_left + 0.5 * GRAVITY * level_left * level_left,
        mass_right * speed_right + 0.5 * GRAVITY * level_right * level_right,
        mass_left,
        mass_right,
    )
    side_flux = riemann_flux(
        mass_left * drift_left,
        mass_right * drift_right,
        level_left * drift_left,
        level_right * drift_right,
    )

    def lower_face(values):
        return take_range(values, 0, -1, direction)

    def upper_face(values):
        return take_range(values, 1, None, direction)

    cell_low = take_range(water_low, 1, -1, direction)
    cell_high = take_range(water_high, 1, -1, direction)
    ground_cell_low = take_range(ground_low, 1, -1, direction)
    ground_cell_high = take_range(ground_high, 1, -1, direction)
    below_level = lower_face(level_right)
    above_level = upper_face(level_left)
    mass_rate = lower_face(mass_flux) - upper_face(mass_flux)
    push_rate = (
        lower_face(push_flux)
        - upper_face(push_flux)
        + 0.5 * GRAVITY * (cell_low * cell_low - below_level * below_level)
        - 0.5 * GRAVITY * (cell_high * cell_high - above_level * above_level)
        + 0.5 * GRAVITY * (cell_low + cell_high) * (ground_cell_low - ground_cell_high)
    )
    side_rate = lower_face(side_flux) - upper_face(side_flux)
    return (mass_rate, push_rate, side_rate)


def advance(state, statics):
    water = state[..., 0, :, :]
    flow_x = state[..., 1, :, :]
    flow_y = state[..., 2, :, :]
    ground = statics[..., 0, :, :]
    active = statics[..., 1, :, :]

    def rows_inner(values):
        return values[..., 2:-2, :]

    def cols_inner(values):
        return values[..., :, 2:-2]

    def center(values):
        return values[..., 2:-2, 2:-2]

    mass_x, push_x, side_x = flux_sweep(
        rows_inner(water), rows_inner(flow_x), rows_inner(flow_y), rows_inner(ground), -1
    )
    mass_y, push_y, side_y = flux_sweep(
        cols_inner(water), cols_inner(flow_y), cols_inner(flow_x), cols_inner(ground), -2
    )
    new_water = center(water) + TIME_STEP * (mass_x + mass_y)
    new_flow_x = center(flow_x) + TIME_STEP * (push_x + side_y)
    new_flow_y = center(flow_y) + TIME_STEP * (side_x + push_y)
    updated = jnp.stack([new_water, new_flow_x, new_flow_y], axis=-3)
    keeping = center(active)[..., None, :, :] > 0.5
    return jnp.where(keeping, updated, center(state))


def cut_tiles(block, pick_rows, pick_cols, extent):

    def one_tile(row_pick, col_pick):
        return lax.dynamic_slice(
            block,
            (jnp.int32(0), row_pick * TILE, col_pick * TILE),
            (block.shape[0], extent, extent),
        )

    return jax.vmap(one_tile)(pick_rows, pick_cols)


def owned_tiles(tile_ids, row_index, col_index, tile_cols_all):
    tile_row = tile_ids // tile_cols_all
    tile_col = tile_ids % tile_cols_all
    inside = (tile_ids >= 0) & (tile_row // RT == row_index) & (tile_col // CT == col_index)
    local_row = jnp.clip(tile_row - row_index * RT, 0, RT - 1)
    local_col = jnp.clip(tile_col - col_index * CT, 0, CT - 1)
    return (inside, local_row, local_col)


def as_column(flags):
    return flags[:, None, None, None]


def shards(depth, velocity, bed, slots):
    half = lax.axis_size("rows") // 2
    row_index = lax.axis_index("rows")
    col_index = lax.axis_index("cols")
    tile_cols_all = CT * lax.axis_size("cols")
    move_count = RT * CT // 2
    listed = slots[0, 0]
    partner_list = passed_along(listed, "rows", half)
    block_rows = jnp.arange(RT, dtype=jnp.int32)[:, None]
    block_cols = jnp.arange(CT, dtype=jnp.int32)[None, :]
    block_ids = (row_index * RT + block_rows) * tile_cols_all + col_index * CT + block_cols
    both_lists = jnp.concatenate([listed, partner_list])
    active_tiles = jnp.any(block_ids[:, :, None] == both_lists[None, None, :], axis=-1).astype(
        jnp.float32
    )
    active_cells = jnp.broadcast_to(active_tiles[:, None, :, None], (RT, TILE, CT, TILE)).reshape(
        RT * TILE, CT * TILE
    )
    state = jnp.stack([depth, depth * velocity[0], depth * velocity[1]])
    statics = jnp.stack([bed, active_cells])
    mine_own, mine_row, mine_col = owned_tiles(listed, row_index, col_index, tile_cols_all)
    send_own, send_row, send_col = owned_tiles(partner_list, row_index, col_index, tile_cols_all)
    send_rank = jnp.cumsum(send_own.astype(jnp.int32)) - 1
    picks = (
        send_own[None, :] & (send_rank[None, :] == jnp.arange(move_count, dtype=jnp.int32)[:, None])
    ).astype(jnp.int32)
    out_rows = jnp.sum(picks * send_row[None, :], axis=1)
    out_cols = jnp.sum(picks * send_col[None, :], axis=1)
    out_valid = jnp.sum(picks, axis=1) > 0
    from_partner = (listed >= 0) & jnp.logical_not(mine_own)
    recv_slot = jnp.clip(jnp.cumsum(from_partner.astype(jnp.int32)) - 1, 0, move_count - 1)
    whole = with_halo(jnp.concatenate([state, statics]), (("rows", 1), ("cols", 2)), 4)
    middle = advance(whole[:3], whole[3:])
    state = advance(middle, whole[3:, 2:-2, 2:-2])
    outgoing = jnp.where(as_column(out_valid), cut_tiles(state, out_rows, out_cols, TILE), 0.0)
    received = passed_along(outgoing, "rows", half)
    own_part = cut_tiles(state, mine_row, mine_col, TILE)
    packed = jnp.where(
        as_column(mine_own), own_part, jnp.where(as_column(from_partner), received[recv_slot], 0.0)
    )
    return packed[None, None]


def solution(mesh):
    in_specs = (
        P(("groups", "rows"), "cols"),
        P(None, ("groups", "rows"), "cols"),
        P(("groups", "rows"), "cols"),
        P(("groups", "rows"), "cols", None),
    )
    out_specs = P(("groups", "rows"), "cols", None, None, None, None)
    return jax.shard_map(shards, mesh=mesh, in_specs=in_specs, out_specs=out_specs, check_vma=False)
```

profile of v0, /device:TPU:0, one launch (start us, length us, event | category | flops | bytes accessed | tf_op | source)
XLA Modules:
  0.0 73.6 jit_solution(3947134042088422195)
XLA Ops:
  0.0 4.1 %collective-permute-start = (s32[3]{0:T(128)}, s32[3]{0:T(128)S(1)}, u32[]{:S(2)}, u32[]{:S(2)}) collective-permute-start(s32[3]{0:T(128)} %bitcast.129), channel_id=1, source_target_pairs={{8,0},{10,2},{12,4},{14,6},{0,8},{2,10},{4,12},{6,14},{9,1},{11,3}... | collective-permute-start | bytes 44 | tf_op jit(solution)/shard_map/ppermute | solution.py:20
  4.2 0.7 compare_select_fusion.4
  4.9 0.7 not_and_fusion
  5.6 1.0 %bitcast_dynamic-update-slice_fusion.5 = f32[5,256,256]{2,1,0:T(8,128)S(1)} fusion(f32[256,256]{1,0:T(8,128)} %param.4), kind=kLoop, calls=%fused_computation.301 | loop fusion | bytes 524288
  6.6 1.1 %bitcast_dynamic-update-slice_fusion.4 = f32[5,256,256]{2,1,0:T(8,128)S(1)} fusion(f32[5,256,256]{2,1,0:T(8,128)S(1)} %bitcast_dynamic-update-slice_fusion.5, f32[256,256]{1,0:T(8,128)} %param.4, f32[2,256,256]{2,1,0:T(8,128)} %param.5), kind=kLoop, calls=%fused_computation.299 | loop fusion | flops 65536 | bytes 786432
  8.8 3.4 %collective-permute-start.1 = (f32[5,4,256]{2,1,0:T(4,128)S(1)}, f32[5,4,256]{2,1,0:T(4,128)S(1)}, u32[]{:S(2)}, u32[]{:S(2)}) collective-permute-start(f32[5,4,256]{2,1,0:T(4,128)S(1)} %get-tuple-element.123), channel_id=1, source_target_pairs={{0,2},{2,4},{4,6},{6,8},{8,10},{10,12},{12,14},{1,3},{3,5},{5,7},{... | collective-permute-start | bytes 61448 | tf_op jit(solution)/shard_map/ppermute | solution.py:31
  12.3 1.3 %collective-permute-start.2 = (f32[5,4,256]{2,1,0:T(4,128)S(1)}, f32[5,4,256]{2,1,0:T(4,128)S(1)}, u32[]{:S(2)}, u32[]{:S(2)}) collective-permute-start(f32[5,4,256]{2,1,0:T(4,128)S(1)} %get-tuple-element.124), channel_id=1, source_target_pairs={{2,0},{4,2},{6,4},{8,6},{10,8},{12,10},{14,12},{3,1},{5,3},{7,5},{... | collective-permute-start | bytes 61448 | tf_op jit(solution)/shard_map/ppermute | solution.py:33
  14.0 4.0 %collective-permute-done.2 = f32[5,4,256]{2,1,0:T(4,128)S(1)} collective-permute-done((f32[5,4,256]{2,1,0:T(4,128)S(1)}, f32[5,4,256]{2,1,0:T(4,128)S(1)}, u32[]{:S(2)}, u32[]{:S(2)}) %collective-permute-start.2) | collective-permute-done | bytes 20512 | tf_op jit(solution)/shard_map/ppermute | solution.py:33
  18.6 1.3 %collective-permute-start.3 = (f32[5,264,4]{1,2,0:T(4,128)S(1)}, f32[5,264,4]{1,2,0:T(4,128)S(1)}, u32[]{:S(2)}, u32[]{:S(2)}) collective-permute-start(f32[5,264,4]{1,2,0:T(4,128)S(1)} %copy.23), channel_id=1, source_target_pairs={{0,1},{2,3},{4,5},{6,7},{8,9},{10,11},{12,13},{14,15},{16,17},{18,... | collective-permute-start | bytes 63368 | tf_op jit(solution)/shard_map/ppermute | solution.py:31
  20.2 1.3 %collective-permute-start.4 = (f32[5,264,4]{1,2,0:T(4,128)S(1)}, f32[5,264,4]{1,2,0:T(4,128)S(1)}, u32[]{:S(2)}, u32[]{:S(2)}) collective-permute-start(f32[5,264,4]{1,2,0:T(4,128)S(1)} %copy.24), channel_id=1, source_target_pairs={{1,0},{3,2},{5,4},{7,6},{9,8},{11,10},{13,12},{15,14},{17,16},{19,... | collective-permute-start | bytes 63368 | tf_op jit(solution)/shard_map/ppermute | solution.py:33
  22.0 1.4 %collective-permute-done.4 = f32[5,264,4]{1,2,0:T(4,128)S(1)} collective-permute-done((f32[5,264,4]{1,2,0:T(4,128)S(1)}, f32[5,264,4]{1,2,0:T(4,128)S(1)}, u32[]{:S(2)}, u32[]{:S(2)}) %collective-permute-start.4) | collective-permute-done | bytes 21152 | tf_op jit(solution)/shard_map/ppermute | solution.py:33
  23.6 0.8 %pad_maximum_fusion = f32[5,264,264]{2,1,0:T(8,128)S(1)} fusion(f32[5,264,4]{2,1,0:T(8,128)S(1)} %copy.26, f32[5,4,256]{2,1,0:T(4,128)S(1)} %collective-permute-done.2, f32[5,256,256]{2,1,0:T(8,128)S(1)} %constant_dynamic-update-slice_fusion, f32[5,4,256]{2,1,0:T(4,128)S(1)} %collective-permute-done.1, f32[5,264,4]{2,1,0:T(8,128)S(1)} %copy.25), kind=kLoop, calls=%fused_computation.5 | loop fusion | flops 1393920 | bytes 2787840 | tf_op jit(solution)/shard_map/concatenate | solution.py:29
  26.5 0.4 slice_subtract_fusion.28
  27.1 0.4 slice_subtract_fusion.29
  28.4 0.4 slice_subtract_fusion.27
  29.1 0.4 slice_subtract_fusion.26
  30.2 1.0 %fusion.61 = (f32[260,261]{1,0:T(8,128)S(1)}, f32[260,261]{1,0:T(8,128)S(1)}, f32[260,261]{1,0:T(8,128)S(1)}, f32[260,261]{1,0:T(8,128)S(1)}, f32[260,261]{1,0:T(8,128)S(1)}) fusion(f32[260,262]{1,0:T(8,128)S(1)} %multiply_multiply_fusion.16, f32[260,262]{1,0:T(8,128)S(1)} %slice.909, f32[260,262]{1,0:T(8,128)S(1)} %get-tuple-element.136, ...), kind=kLoop, calls=%fused_computation.135 | loop fusion | flops 2917980 | bytes 3528720 | tf_op jit(solution)/shard_map/div | solution.py:95
  31.3 1.1 %fusion.5 = (f32[260,261]{1,0:T(8,128)S(1)}, f32[260,261]{1,0:T(8,128)S(1)}) fusion(f32[260,261]{1,0:T(8,128)S(1)} %get-tuple-element.94, f32[260,261]{1,0:T(8,128)S(1)} %get-tuple-element.93, f32[260,261]{1,0:T(8,128)S(1)} %get-tuple-element.92, f32[260,261]{1,0:T(8,128)S(1)} %get-tuple-element.91, f32[260,262]{1,0:T(8,128)S(1)} %multiply_multiply_fusion.8, ...), kind=kLoop, calls=%fused_computation.31 | loop fusion | flops 3732300 | bytes 3257280 | tf_op jit(solution)/shard_map/div | solution.py:95
  32.3 0.9 %fusion.62 = (f32[261,260]{1,0:T(8,128)S(1)}, f32[261,260]{1,0:T(8,128)S(1)}, f32[261,260]{1,0:T(8,128)S(1)}, f32[261,260]{1,0:T(8,128)S(1)}, f32[261,260]{1,0:T(8,128)S(1)}) fusion(f32[262,260]{1,0:T(8,128)S(1)} %multiply_multiply_fusion.13, f32[262,260]{1,0:T(8,128)S(1)} %slice.936, f32[262,260]{1,0:T(8,128)S(1)} %get-tuple-element.138, ...), kind=kLoop, calls=%fused_computation.138 | loop fusion | flops 2917980 | bytes 3528720 | tf_op jit(solution)/shard_map/div | solution.py:95
  33.3 1.1 %add_divide_fusion.1 = (f32[261,260]{1,0:T(8,128)S(1)}, f32[261,260]{1,0:T(8,128)S(1)}) fusion(f32[261,260]{1,0:T(8,128)S(1)} %get-tuple-element.99, f32[261,260]{1,0:T(8,128)S(1)} %get-tuple-element.98, f32[262,260]{1,0:T(8,128)S(1)} %multiply_multiply_fusion.9, f32[262,260]{1,0:T(8,128)S(1)} %slice.966, f32[261,260]{1,0:T(8,128)S(1)} %get-tuple-element.97, ...), kind=kLoop, calls=%fused_computation.130 | loop fusion | flops 3732300 | bytes 3257280 | tf_op jit(solution)/shard_map/div | solution.py:95
  34.3 0.8 %fusion.34 = f32[1,260,260]{2,1,0:T(8,128)S(1)} fusion(f32[261,260]{1,0:T(8,128)S(1)} %get-tuple-element.117, f32[260,262]{1,0:T(8,128)S(1)} %get-tuple-element.134, f32[260,262]{1,0:T(8,128)S(1)} %get-tuple-element.133, f32[260,261]{1,0:T(8,128)S(1)} %get-tuple-element.94, f32[260,261]{1,0:T(8,128)S(1)} %get-tuple-element.93, ...), kind=kLoop, calls=%fused_computation.74 | loop fusion | flops 1352000 | bytes 3244800 | tf_op jit(solution)/shard_map/stack | solution.py:166
  35.2 0.9 %fusion.20 = (f32[1,260,260]{2,1,0:T(8,128)S(1)}, f32[1,260,260]{2,1,0:T(8,128)S(1)}) fusion(f32[262,260]{1,0:T(8,128)S(1)} %get-tuple-element.140, f32[262,260]{1,0:T(8,128)S(1)} %get-tuple-element.139, f32[261,260]{1,0:T(8,128)S(1)} %get-tuple-element.99, f32[261,260]{1,0:T(8,128)S(1)} %get-tuple-element.98, f32[261,260]{1,0:T(8,128)S(1)} %get-tuple-element.118, ...), kind=kLoop, calls=%fused_computation.51 | loop fusion | flops 1690000 | bytes 4867200 | tf_op jit(solution)/shard_map/stack | solution.py:166
  36.1 0.5 slice_select_fusion
  38.7 0.4 slice_subtract_fusion.31
  39.6 0.4 slice_subtract_fusion.30
  41.8 1.0 %fusion.81 = (f32[256,257]{1,0:T(8,128)S(1)}, f32[256,257]{1,0:T(8,128)S(1)}, f32[256,257]{1,0:T(8,128)S(1)}, f32[256,257]{1,0:T(8,128)S(1)}, f32[256,257]{1,0:T(8,128)S(1)}) fusion(f32[256,258]{1,0:T(8,128)S(1)} %multiply_multiply_fusion.22, f32[256,258]{1,0:T(8,128)S(1)} %slice.1009, f32[256,258]{1,0:T(8,128)S(1)} %get-tuple-element.144, ...), kind=kLoop, calls=%fused_computation.191 | loop fusion | flops 2829056 | bytes 3421184 | tf_op jit(solution)/shard_map/div | solution.py:95
  42.8 0.6 fusion.98
  43.6 1.0 %fusion.68 = (f32[256,257]{1,0:T(8,128)S(1)}, f32[256,257]{1,0:T(8,128)S(1)}) fusion(f32[256,257]{1,0:T(8,128)S(1)} %get-tuple-element.84, f32[256,257]{1,0:T(8,128)S(1)} %get-tuple-element.83, f32[256,257]{1,0:T(8,128)S(1)} %get-tuple-element.82, f32[256,257]{1,0:T(8,128)S(1)} %get-tuple-element.81, f32[256,258]{1,0:T(8,128)S(1)} %multiply_multiply_fusion.18, ...), kind=kLoop, calls=%fused_computation.163 | loop fusion | flops 3618560 | bytes 3158016 | tf_op jit(solution)/shard_map/div | solution.py:95
  44.6 0.7 add_divide_fusion.3
  45.3 0.6 fusion.114
  45.9 0.4 fusion.104
  46.6 0.7 copy-done.2
  47.3 4.1 %while.5 = (s32[]{:T(128)}, f32[3,256,256]{2,1,0:T(8,128)S(1)}, s32[2,3]{1,0:T(2,128)S(1)}, f32[2,3,128,128]{3,2,1,0:T(8,128)S(1)}) while((s32[]{:T(128)}, f32[3,256,256]{2,1,0:T(8,128)S(1)}, s32[2,3]{1,0:T(2,128)S(1)}, f32[2,3,128,128]{3,2,1,0:T(8,128)S(1)}) %tuple.108), condition=%wide.while_cond.1.clone, body=%wide.while_body.1.sunk.clone | while | flops 2 | bytes 393325 | solution.py:174
  47.3 0.6 fusion.147
  47.9 1.4 %bitcast_dynamic-update-slice_fusion.11 = f32[2,3,128,128]{3,2,1,0:T(8,128)S(1)} fusion(f32[2,3,128,128]{3,2,1,0:T(8,128)S(1)} %get-tuple-element.244, s32[]{:T(128)} %get-tuple-element.241, f32[3,256,256]{2,1,0:T(8,128)S(1)} %get-tuple-element.246, s32[]{:T(128)} %bitcast.127, s32[]{:T(128)} %bitcast.128), kind=kLoop, calls=%fused_computation.3.clone.1.clone | loop fusion | bytes 393228 | tf_op jit(solution)/shard_map/vmap()/gather
  49.3 0.6 fusion.147
  49.9 1.4 %bitcast_dynamic-update-slice_fusion.11 = f32[2,3,128,128]{3,2,1,0:T(8,128)S(1)} fusion(f32[2,3,128,128]{3,2,1,0:T(8,128)S(1)} %get-tuple-element.244, s32[]{:T(128)} %get-tuple-element.241, f32[3,256,256]{2,1,0:T(8,128)S(1)} %get-tuple-element.246, s32[]{:T(128)} %bitcast.127, s32[]{:T(128)} %bitcast.128), kind=kLoop, calls=%fused_computation.3.clone.1.clone | loop fusion | bytes 393228 | tf_op jit(solution)/shard_map/vmap()/gather
  51.4 0.7 collective-permute-start.5
  52.2 6.5 %while.4 = (s32[]{:T(128)}, f32[3,256,256]{2,1,0:T(8,128)S(1)}, s32[3,3]{1,0:T(4,128)S(1)}, f32[3,3,128,128]{3,2,1,0:T(8,128)S(1)}) while((s32[]{:T(128)}, f32[3,256,256]{2,1,0:T(8,128)S(1)}, s32[3,3]{1,0:T(4,128)S(1)}, f32[3,3,128,128]{3,2,1,0:T(8,128)S(1)}) %tuple.107), condition=%wide.while_cond.clone, body=%wide.while_body.sunk.clone | while | flops 2 | bytes 393325 | solution.py:174
  52.2 0.7 fusion.146
  52.8 1.5 %bitcast_dynamic-update-slice_fusion.10 = f32[3,3,128,128]{3,2,1,0:T(8,128)S(1)} fusion(f32[3,3,128,128]{3,2,1,0:T(8,128)S(1)} %get-tuple-element.256, s32[]{:T(128)} %get-tuple-element.253, f32[3,256,256]{2,1,0:T(8,128)S(1)} %get-tuple-element.258, s32[]{:T(128)} %bitcast.124, s32[]{:T(128)} %bitcast.125), kind=kLoop, calls=%fused_computation.1.clone.1.clone | loop fusion | bytes 393228 | tf_op jit(solution)/shard_map/vmap()/gather
  54.3 0.7 fusion.146
  55.0 1.5 %bitcast_dynamic-update-slice_fusion.10 = f32[3,3,128,128]{3,2,1,0:T(8,128)S(1)} fusion(f32[3,3,128,128]{3,2,1,0:T(8,128)S(1)} %get-tuple-element.256, s32[]{:T(128)} %get-tuple-element.253, f32[3,256,256]{2,1,0:T(8,128)S(1)} %get-tuple-element.258, s32[]{:T(128)} %bitcast.124, s32[]{:T(128)} %bitcast.125), kind=kLoop, calls=%fused_computation.1.clone.1.clone | loop fusion | bytes 393228 | tf_op jit(solution)/shard_map/vmap()/gather
  56.5 0.7 fusion.146
  57.2 1.5 %bitcast_dynamic-update-slice_fusion.10 = f32[3,3,128,128]{3,2,1,0:T(8,128)S(1)} fusion(f32[3,3,128,128]{3,2,1,0:T(8,128)S(1)} %get-tuple-element.256, s32[]{:T(128)} %get-tuple-element.253, f32[3,256,256]{2,1,0:T(8,128)S(1)} %get-tuple-element.258, s32[]{:T(128)} %bitcast.124, s32[]{:T(128)} %bitcast.125), kind=kLoop, calls=%fused_computation.1.clone.1.clone | loop fusion | bytes 393228 | tf_op jit(solution)/shard_map/vmap()/gather
  58.6 13.4 %collective-permute-done.5 = f32[2,3,128,128]{3,2,1,0:T(8,128)S(1)} collective-permute-done((f32[2,3,128,128]{3,2,1,0:T(8,128)S(1)}, f32[2,3,128,128]{3,2,1,0:T(8,128)S(1)}, u32[]{:S(2)}, u32[]{:S(2)}) %collective-permute-start.5) | collective-permute-done | bytes 393248 | tf_op jit(solution)/shard_map/ppermute | solution.py:20
  72.0 0.6 gather_fusion
  72.6 1.0 %fusion = f32[1,1,3,3,128,128]{5,4,3,2,1,0:T(8,128)} fusion(f32[3,3,128,128]{3,2,1,0:T(8,128)S(1)} %gather_fusion, f32[3,3,128,128]{3,2,1,0:T(8,128)S(1)} %get-tuple-element.12, pred[3]{0:T(512)(128)(4,1)S(1)} %get-tuple-element.72, pred[3]{0:T(512)(128)(4,1)S(1)} %get-tuple-element.73), kind=kLoop, calls=%fused_computation.22 | loop fusion | flops 294912 | bytes 1769478 | tf_op jit(solution)/shard_map/jit(_where)/select_n | solution.py:233
  (98 shorter events, 12.3 us)
Async XLA Ops:
  0.0 7.7 %copy-start.4 = (s32[1,1,3]{2,1,0:T(1,128)S(1)}, s32[1,1,3]{2,1,0:T(1,128)}, u32[]{:S(2)}) copy-start(s32[1,1,3]{2,1,0:T(1,128)} %param.7) | copy-start | bytes 40
  0.0 7.7 %copy-start = (f32[256,256]{1,0:T(8,128)S(1)}, f32[256,256]{1,0:T(8,128)}, u32[]{:S(2)}) copy-start(f32[256,256]{1,0:T(8,128)} %param.4) | copy-start | bytes 786436
  0.0 7.7 %copy-start.1 = (f32[2,256,256]{2,1,0:T(8,128)S(1)}, f32[2,256,256]{2,1,0:T(8,128)}, u32[]{:S(2)}) copy-start(f32[2,256,256]{2,1,0:T(8,128)} %param.5) | copy-start | bytes 1572868
  0.0 8.1 %copy-start.3 = (f32[256,256]{1,0:T(8,128)S(1)}, f32[256,256]{1,0:T(8,128)}, u32[]{:S(2)}) copy-start(f32[256,256]{1,0:T(8,128)} %param.6) | copy-start | bytes 786436
  0.0 8.1 %collective-permute-start = (s32[3]{0:T(128)}, s32[3]{0:T(128)S(1)}, u32[]{:S(2)}, u32[]{:S(2)}) collective-permute-start(s32[3]{0:T(128)} %bitcast.129), channel_id=1, source_target_pairs={{8,0},{10,2},{12,4},{14,6},{0,8},{2,10},{4,12},{6,14},{9,1},{11,3}... | collective-permute-start | bytes 44 | tf_op jit(solution)/shard_map/ppermute | solution.py:20
  8.8 5.1 %collective-permute-start.1 = (f32[5,4,256]{2,1,0:T(4,128)S(1)}, f32[5,4,256]{2,1,0:T(4,128)S(1)}, u32[]{:S(2)}, u32[]{:S(2)}) collective-permute-start(f32[5,4,256]{2,1,0:T(4,128)S(1)} %get-tuple-element.123), channel_id=1, source_target_pairs={{0,2},{2,4},{4,6},{6,8},{8,10},{10,12},{12,14},{1,3},{3,5},{5,7},{... | collective-permute-start | bytes 61448 | tf_op jit(solution)/shard_map/ppermute | solution.py:31
  12.3 5.7 %collective-permute-start.2 = (f32[5,4,256]{2,1,0:T(4,128)S(1)}, f32[5,4,256]{2,1,0:T(4,128)S(1)}, u32[]{:S(2)}, u32[]{:S(2)}) collective-permute-start(f32[5,4,256]{2,1,0:T(4,128)S(1)} %get-tuple-element.124), channel_id=1, source_target_pairs={{2,0},{4,2},{6,4},{8,6},{10,8},{12,10},{14,12},{3,1},{5,3},{7,5},{... | collective-permute-start | bytes 61448 | tf_op jit(solution)/shard_map/ppermute | solution.py:33
  18.6 3.1 %collective-permute-start.3 = (f32[5,264,4]{1,2,0:T(4,128)S(1)}, f32[5,264,4]{1,2,0:T(4,128)S(1)}, u32[]{:S(2)}, u32[]{:S(2)}) collective-permute-start(f32[5,264,4]{1,2,0:T(4,128)S(1)} %copy.23), channel_id=1, source_target_pairs={{0,1},{2,3},{4,5},{6,7},{8,9},{10,11},{12,13},{14,15},{16,17},{18,... | collective-permute-start | bytes 63368 | tf_op jit(solution)/shard_map/ppermute | solution.py:31
  20.2 3.1 %collective-permute-start.4 = (f32[5,264,4]{1,2,0:T(4,128)S(1)}, f32[5,264,4]{1,2,0:T(4,128)S(1)}, u32[]{:S(2)}, u32[]{:S(2)}) collective-permute-start(f32[5,264,4]{1,2,0:T(4,128)S(1)} %copy.24), channel_id=1, source_target_pairs={{1,0},{3,2},{5,4},{7,6},{9,8},{11,10},{13,12},{15,14},{17,16},{19,... | collective-permute-start | bytes 63368 | tf_op jit(solution)/shard_map/ppermute | solution.py:33
  46.3 1.0 %copy-start.2 = (f32[2,3,128,128]{3,2,1,0:T(8,128)S(1)}, f32[2,3,128,128]{3,2,1,0:T(8,128)}, u32[]{:S(2)}) copy-start(f32[2,3,128,128]{3,2,1,0:T(8,128)} %custom-call.5) | copy-start | bytes 1179652
  51.4 20.6 %collective-permute-start.5 = (f32[2,3,128,128]{3,2,1,0:T(8,128)S(1)}, f32[2,3,128,128]{3,2,1,0:T(8,128)S(1)}, u32[]{:S(2)}, u32[]{:S(2)}) collective-permute-start(f32[2,3,128,128]{3,2,1,0:T(8,128)S(1)} %broadcast_select_fusion), channel_id=1, source_target_pairs={{8,0},{10,2},{12,4},{14,6},{0,8},{2,10},{4,12},{6,14},{9,1},{11,3}... | collective-permute-start | bytes 1179656 | tf_op jit(solution)/shard_map/ppermute | solution.py:20
where the time goes:
time: 74 us; the launch traced here: 73.6 us
  other arithmetic  25.1 us (34%)
  waiting for transfers between devices  18.8 us (25%)
  local copies, waits for them, and re-layouts  16.8 us (23%)
  starting transfers between devices  12.2 us (16%)
    ppermute x2, waiting for transfers between devices, passed_along(): return lax.ppermute(block, axis, route)  13.4 us
    gather x15, local copies, waits for them, and re-layouts  10.4 us
    div x8, other arithmetic, riemann_flux(): (upper_speed * flux_left - lower_speed * flux_right + upper_speed * lower...  7.36 us
    ppermute x2, waiting for transfers between devices, with_halo(): lax.ppermute(head, axis, [((i + 1) % count, i) for i in range(ends)])  5.36 us
    ppermute x2, starting transfers between devices, passed_along(): return lax.ppermute(block, axis, route)  4.85 us
    ppermute x2, starting transfers between devices, with_halo(): lax.ppermute(tail, axis, [(i, (i + 1) % count) for i in range(ends)])  4.73 us
    sub x16, other arithmetic, face_values(): take_range(values, 1, None, direction)  3.29 us
    another operation x5, other arithmetic, advance(): updated = jnp.stack([new_water, new_flow_x, new_flow_y], axis=-3)  2.9 us
  transfers between devices with their start and end apart: 6, of which 3 were waited for; matrix products, arithmetic and copies ran while one was open for 15% of the time, Pallas kernels for 0%

commit v1 on v0

v1 whole, which is shorter than its diff:
```python
import jax
import jax.numpy as jnp
from jax import lax
from jax.experimental import pallas as pl
from jax.experimental.pallas import tpu as pltpu
from jax.sharding import PartitionSpec as P

TILE = 128
RT = 2
CT = 2
SLOTS = 3
MOVED = RT * CT // 2
ROWS = RT * TILE
COLS = CT * TILE
PAD = 16
DEEP = ROWS + 2 * PAD
SEAM = 24
SEAM_DEEP = SEAM + 2 * PAD
REACH = 4

GRAVITY = 9.81
TIME_STEP = 0.04
DRY_DEPTH = 0.05
SPEED_FLOOR = 0.5
ROOT_GRAVITY = GRAVITY**0.5
TINY = 1.2e-38

VMEM = pl.BlockSpec(memory_space=pltpu.VMEM)
SMEM = pl.BlockSpec(memory_space=pltpu.SMEM)


def f32(*shape):
    return jax.ShapeDtypeStruct(shape, jnp.float32)


def call(kernel, name, ins, outs, scratch=(), **extra):
    return pl.pallas_call(
        kernel,
        name=name,
        in_specs=list(ins),
        out_specs=tuple(VMEM for _ in outs),
        out_shape=tuple(outs),
        scratch_shapes=list(scratch),
        compiler_params=pltpu.CompilerParams(vmem_limit_bytes=20 * 2**20),
        **extra,
    )


def limited(down, up):
    return 0.5 * jnp.maximum(jnp.minimum(down, jnp.maximum(up, 0.0)), jnp.minimum(up, 0.0))


def speeds(water, normal, across):
    square = water * water
    factor = (water + water) / (square + jnp.maximum(square, DRY_DEPTH * DRY_DEPTH))
    return factor * normal, factor * across


def wave_speed(level):
    return (ROOT_GRAVITY * level) * lax.rsqrt(jnp.maximum(level, TINY))


def face_flux(left, right):
    water_l, speed_l, drift_l, ground_l = left
    water_r, speed_r, drift_r, ground_r = right
    top = jnp.maximum(ground_l, ground_r)
    level_l = jnp.maximum(water_l + (ground_l - top), 0.0)
    level_r = jnp.maximum(water_r + (ground_r - top), 0.0)
    wave_l = wave_speed(level_l)
    wave_r = wave_speed(level_r)
    lower = jnp.minimum(jnp.minimum(speed_l - wave_l, speed_r - wave_r), 0.0)
    upper = jnp.maximum(jnp.maximum(speed_l + wave_l, speed_r + wave_r), 0.0)
    inverse = 1.0 / jnp.maximum(upper - lower, SPEED_FLOOR)
    up = upper * inverse
    low = lower * inverse
    both = upper * low
    part_l = level_l * (up * speed_l - both)
    part_r = level_r * (both - low * speed_r)
    press_l = (0.5 * GRAVITY) * (level_l * level_l)
    press_r = (0.5 * GRAVITY) * (level_r * level_r)
    mass = part_l + part_r
    push = part_l * speed_l + part_r * speed_r + up * press_l - low * press_r
    side = part_l * drift_l + part_r * drift_r
    return mass, push - press_l, push - press_r, side


def sweep(src, dst, width, steps, src_row, dst_row, lane_flow, row_flow):
    lane = lax.broadcasted_iota(jnp.int32, (8, 128), 1)
    sub = lax.broadcasted_iota(jnp.int32, (8, 128), 0)
    cols = range(width)

    def from_lower(values):
        turned = [pltpu.roll(v, 1, 1) for v in values]
        return [jnp.where(lane == 0, turned[w - 1], turned[w]) for w in cols]

    def from_upper(values):
        turned = [pltpu.roll(v, 127, 1) for v in values]
        return [jnp.where(lane == 127, turned[(w + 1) % width], turned[w]) for w in cols]

    def step(i, carry):
        shift = pl.multiple_of(i * 8, 8)
        row = shift + src_row
        x = [[src[f, w, pl.ds(row, 8), :] for w in cols] for f in range(4)]
        low, high, half = [], [], []
        for f in (0, lane_flow, row_flow, 3):
            before = from_lower(x[f])
            down = [x[f][w] - before[w] for w in cols]
            up = from_upper(down)
            hs = [limited(down[w], up[w]) for w in cols]
            low.append([x[f][w] - hs[w] for w in cols])
            high.append([x[f][w] + hs[w] for w in cols])
            half.append(hs)
        fast = [speeds(high[0][w], high[1][w], high[2][w]) for w in cols]
        slow = [speeds(low[0][w], low[1][w], low[2][w]) for w in cols]
        left = [
            from_lower(high[0]),
            from_lower([v[0] for v in fast]),
            from_lower([v[1] for v in fast]),
            from_lower(high[3]),
        ]
        flux = [
            face_flux([left[k][w] for k in range(4)], (low[0][w], slow[w][0], slow[w][1], low[3][w]))
            for w in cols
        ]
        mass_up = from_upper([v[0] for v in flux])
        push_up = from_upper([v[1] for v in flux])
        side_up = from_upper([v[3] for v in flux])
        now = []
        for w in cols:
            weight = (2.0 * GRAVITY) * x[0][w]
            gain_water = flux[w][0] - mass_up[w]
            gain_lane = flux[w][2] - push_up[w] - weight * (half[0][w] + half[3][w])
            gain_row = flux[w][3] - side_up[w]
            low_r, high_r, half_r = [], [], []
            for f in (0, row_flow, lane_flow, 3):
                before = src[f, w, pl.ds(row - 1, 8), :]
                after = src[f, w, pl.ds(row + 1, 8), :]
                hs = limited(x[f][w] - before, after - x[f][w])
                low_r.append(x[f][w] - hs)
                high_r.append(x[f][w] + hs)
                half_r.append(hs)
            fast_n, fast_t = speeds(high_r[0], high_r[1], high_r[2])
            slow_n, slow_t = speeds(low_r[0], low_r[1], low_r[2])
            old_high, old_flux, old_gain = carry[w]
            high_now = tuple(pltpu.roll(v, 1, 0) for v in (high_r[0], fast_n, fast_t, high_r[3]))
            left_r = [jnp.where(sub == 0, o, n) for o, n in zip(old_high, high_now)]
            mass, push_l, push_r, side = face_flux(left_r, (low_r[0], slow_n, slow_t, low_r[3]))
            gain = (
                gain_water + mass,
                gain_lane + side,
                gain_row + push_r - weight * (half_r[0] + half_r[3]),
            )
            flux_now = tuple(pltpu.roll(v, 7, 0) for v in (mass, side, push_l))
            out = shift + (dst_row - 8)
            for f, g, o, n in zip((0, lane_flow, row_flow), old_gain, old_flux, flux_now):
                kept = src[f, w, pl.ds(row - 8, 8), :]
                dst[f, w, pl.ds(out, 8), :] = kept + TIME_STEP * (g - jnp.where(sub == 7, n, o))
            now.append((high_now, flux_now, gain))
        return tuple(now)

    zero = jnp.zeros((8, 128), jnp.float32)
    start = tuple(((zero,) * 4, (zero,) * 3, (zero,) * 3) for _ in cols)
    lax.fori_loop(0, steps, step, start)


def load_kernel(depth, velocity, bed, state, moved):
    blank = jnp.zeros((8, TILE), jnp.float32)
    for w in range(CT):
        cols = slice(w * TILE, (w + 1) * TILE)
        for f in range(4):
            for r in (0, 8, PAD + ROWS, PAD + ROWS + 8):
                state[f, w, r : r + 8, :] = blank
                moved[f, w, r : r + 8, :] = blank
        for r in range(0, ROWS, 8):
            rows = slice(r, r + 8)
            held = slice(PAD + r, PAD + r + 8)
            water = depth[rows, cols]
            ground = bed[rows, cols]
            state[0, w, held, :] = water
            state[1, w, held, :] = water * velocity[0, rows, cols]
            state[2, w, held, :] = water * velocity[1, rows, cols]
            state[3, w, held, :] = ground
            moved[3, w, held, :] = ground
    sweep(state, moved, CT, ROWS // 8 + 1, PAD, PAD, 1, 2)


class Lists:
    def __init__(self, listed, partner):
        self.rows = lax.axis_index("rows")
        self.cols = lax.axis_index("cols")
        self.span = CT * lax.axis_size("cols")
        self.ids = [
            (self.rows * RT + t // CT) * self.span + self.cols * CT + t % CT for t in range(RT * CT)
        ]
        self.listed = [listed[k] for k in range(SLOTS)]
        self.partner = [partner[k] for k in range(SLOTS)]

    def inside(self, entry):
        found = [entry == i for i in self.ids]
        any_found = found[0]
        local = jnp.int32(0)
        for t in range(1, RT * CT):
            any_found = any_found | found[t]
            local = jnp.where(found[t], jnp.int32(t), local)
        return any_found, local

    def active(self, t):
        hit = self.listed[0] == self.ids[t]
        for entry in self.listed[1:] + self.partner:
            hit = hit | (entry == self.ids[t])
        return hit

    def outgoing(self):
        used = [jnp.bool_(False)] * MOVED
        tile = [jnp.int32(0)] * MOVED
        rank = jnp.int32(0)
        for entry in self.partner:
            own, local = self.inside(entry)
            for k in range(MOVED):
                take = own & (rank == k)
                used[k] = used[k] | take
                tile[k] = jnp.where(take, local, tile[k])
            rank = rank + own.astype(jnp.int32)
        return used, tile


def send_kernel(listed, partner, state, guess, moved, outgoing, final):
    lists = Lists(listed, partner)
    for t in range(RT * CT):
        rows = slice(PAD + (t // CT) * TILE, PAD + (t // CT + 1) * TILE)

        @pl.when(lists.active(t))
        def _(t=t, rows=rows):
            for f in range(3):
                moved[f, t % CT, rows, :] = guess[f, t % CT, rows, :]

        @pl.when(jnp.logical_not(lists.active(t)))
        def _(t=t, rows=rows):
            for f in range(3):
                moved[f, t % CT, rows, :] = state[f, t % CT, rows, :]

    blank = jnp.zeros((8, TILE), jnp.float32)
    for w in range(CT):
        for f in range(4):
            for r in (0, 8, PAD + ROWS, PAD + ROWS + 8):
                moved[f, w, r : r + 8, :] = blank
        moved[3, w, PAD : PAD + ROWS, :] = state[3, w, PAD : PAD + ROWS, :]
    used, tile = lists.outgoing()
    for r in range(RT):
        needed = jnp.bool_(False)
        for k in range(MOVED):
            needed = needed | (used[k] & (tile[k] // CT == r))

        @pl.when(needed)
        def _(r=r):
            sweep(moved, final.at[r], CT, TILE // 8 + 2, PAD + r * TILE - 8, PAD - 8, 1, 2)

    for k in range(MOVED):
        r = tile[k] // CT
        c = tile[k] % CT
        for f in range(3):
            for b in range(0, TILE, 8):
                outgoing[k, f, b : b + 8, :] = final[r, f, c, PAD + b : PAD + b + 8, :]


def keep_kernel(listed, partner, moved, final):
    lists = Lists(listed, partner)
    used, tile = lists.outgoing()
    for r in range(RT):
        sent = jnp.bool_(False)
        for k in range(MOVED):
            sent = sent | (used[k] & (tile[k] // CT == r))
        own = jnp.bool_(False)
        for entry in lists.listed:
            inside, local = lists.inside(entry)
            own = own | (inside & (local // CT == r))

        @pl.when(own & jnp.logical_not(sent))
        def _(r=r):
            sweep(moved, final.at[r], CT, TILE // 8 + 2, PAD + r * TILE - 8, PAD - 8, 1, 2)


def edge_kernel(listed, partner, state, strips):
    lists = Lists(listed, partner)
    lane = lax.broadcasted_iota(jnp.int32, (TILE, TILE), 1)
    last = slice(PAD + ROWS - 8, PAD + ROWS)
    for f in range(4):
        for w in range(CT):
            cols = slice(w * TILE, (w + 1) * TILE)
            strips[f, 0:8, cols] = state[f, w, last, :]
            strips[f, 8:16, cols] = state[f, w, PAD : PAD + 8, :]
        for r in range(RT):
            rows = slice(PAD + r * TILE, PAD + (r + 1) * TILE)
            ends = jnp.where(lane < TILE // 2, state[f, 0, rows, :], state[f, CT - 1, rows, :])
            turned = ends.T
            cols = slice(r * TILE, (r + 1) * TILE)
            strips[f, 16:24, cols] = turned[TILE - 8 :, :]
            strips[f, 24:32, cols] = turned[:8, :]
    flags = [jnp.where(lists.active(t), 1.0, 0.0) for t in range(RT * CT)]
    for w in range(CT):
        cols = slice(w * TILE, (w + 1) * TILE)
        strips[4, 0:8, cols] = jnp.full((8, TILE), flags[(RT - 1) * CT + w], jnp.float32)
        strips[4, 8:16, cols] = jnp.full((8, TILE), flags[w], jnp.float32)
    for r in range(RT):
        cols = slice(r * TILE, (r + 1) * TILE)
        strips[4, 16:24, cols] = jnp.full((8, TILE), flags[r * CT + CT - 1], jnp.float32)
        strips[4, 24:32, cols] = jnp.full((8, TILE), flags[r * CT], jnp.float32)


def wide_kernel(mine, other, out):
    is_left = lax.axis_index("cols") == 0
    for f in range(5):
        own = jnp.where(is_left, mine[f, 8:12, :], mine[f, 4:8, :])
        near = jnp.where(is_left, other[f, 8:12, :], other[f, 4:8, :])
        out[4 * f : 4 * f + 4, 0:COLS] = jnp.where(is_left, own, near)
        out[4 * f : 4 * f + 4, COLS : 2 * COLS] = jnp.where(is_left, near, own)
    out[20:24, :] = jnp.zeros((4, 2 * COLS), jnp.float32)


def still(dst, src, width):
    for w in range(width):
        rows = slice(PAD, PAD + SEAM)
        alive = src[4, w, rows, :] > 0.5
        for f in range(3):
            dst[f, w, rows, :] = jnp.where(alive, dst[f, w, rows, :], src[f, w, rows, :])


def seam_kernel(listed, partner, mine, other, came, near, fixes, sent, flat, flat2, flat3, tall, tall2, tall3):
    lists = Lists(listed, partner)
    is_left = lists.cols == 0
    lane = lax.broadcasted_iota(jnp.int32, (8, TILE), 1)
    lane4 = lax.broadcasted_iota(jnp.int32, (4, TILE), 1)
    beside = jnp.where(is_left, lane, TILE - 1 - lane) < REACH
    beside4 = jnp.where(is_left, lane4, TILE - 1 - lane4) < REACH
    blank = jnp.zeros((8, TILE), jnp.float32)
    for buffer, width in ((flat, CT + 1), (tall, CT), (flat2, CT + 1), (tall2, CT)):
        for f in range(buffer.shape[0]):
            for w in range(width):
                for r in (0, 8, PAD + SEAM, PAD + SEAM + 8):
                    buffer[f, w, r : r + 8, :] = blank
    for f in range(5):
        for w in range(CT):
            cols = slice(w * TILE, (w + 1) * TILE)
            flat[f, w, PAD : PAD + 8, :] = mine[f, 0:8, cols]
            flat[f, w, PAD + 16 : PAD + 24, :] = mine[f, 8:16, cols]
            tall[f, w, PAD : PAD + 8, :] = mine[f, 16:24, cols]
            tall[f, w, PAD + 16 : PAD + 24, :] = mine[f, 24:32, cols]
            tall[f, w, PAD + 8 : PAD + 12, :] = jnp.where(is_left, other[f, 24:28, cols], 0.0)
            tall[f, w, PAD + 12 : PAD + 16, :] = jnp.where(is_left, 0.0, other[f, 20:24, cols])
        for r, base in ((0, 0), (8, 16)):
            piece = jnp.where(is_left, other[f, r : r + 8, 0:TILE], other[f, r : r + 8, COLS - TILE : COLS])
            flat[f, CT, PAD + base : PAD + base + 8, :] = jnp.where(beside, piece, 0.0)
        rows = slice(4 * f, 4 * f + 4)
        for place, upper in ((8, False), (12, True)):
            halo = jnp.where(is_left == upper, came[rows, :], near[rows, :])
            held = slice(PAD + place, PAD + place + 4)
            for w in range(CT):
                a = halo[:, w * TILE : (w + 1) * TILE]
                b = halo[:, COLS + w * TILE : COLS + (w + 1) * TILE]
                flat[f, w, held, :] = jnp.where(is_left, a, b)
            piece = jnp.where(is_left, halo[:, COLS : COLS + TILE], halo[:, COLS - TILE : COLS])
            flat[f, CT, held, :] = jnp.where(beside4, piece, 0.0)
    for start, middle, end, width, lane_flow, row_flow in (
        (flat, flat2, flat3, CT + 1, 1, 2),
        (tall, tall2, tall3, CT, 2, 1),
    ):
        sweep(start, middle, width, SEAM // 8 + 1, PAD, PAD, lane_flow, row_flow)
        still(middle, start, width)
        for w in range(width):
            middle[3, w, PAD : PAD + SEAM, :] = start[3, w, PAD : PAD + SEAM, :]
        sweep(middle, end, width, SEAM // 8 + 1, PAD, PAD, lane_flow, row_flow)
    for t in range(RT * CT):
        r, c = t // CT, t % CT
        for f in range(3):
            a = PAD + (16 if r == 0 else 4)
            b = PAD + (16 if c == 0 else 4)
            fixes[t, f, 0:4, :] = flat3[f, c, a : a + 4, :]
            fixes[t, f, 4:8, :] = tall3[f, r, b : b + 4, :]
    used, tile = lists.outgoing()
    for k in range(MOVED):
        for f in range(3):
            sent[k, f] = fixes[tile[k], f]


def pack_kernel(listed, partner, early, late, fixes, received, patches, packed, board):
    lists = Lists(listed, partner)
    used, tile = lists.outgoing()
    lane = lax.broadcasted_iota(jnp.int32, (8, TILE), 1)
    sub = lax.broadcasted_iota(jnp.int32, (8, TILE), 0)
    board[...] = jnp.zeros_like(board)
    rank = jnp.int32(0)
    for s in range(SLOTS):
        entry = lists.listed[s]
        own, local = lists.inside(entry)
        foreign = (entry >= 0) & jnp.logical_not(own)
        row = lax.rem(lax.div(jnp.maximum(entry, 0), lists.span), RT)
        col = lax.rem(jnp.maximum(entry, 0), CT)
        swept = jnp.bool_(False)
        for k in range(MOVED):
            swept = swept | (used[k] & (tile[k] // CT == row))
        slot = jnp.minimum(rank, MOVED - 1)
        rank = rank + foreign.astype(jnp.int32)

        def put(cell, fix, s=s, row=row, col=col):
            for f in range(3):
                board[8 * f : 8 * f + 8, :] = fix(f)
            turned = board[...].T
            for f in range(3):
                shift = jnp.where(col == 0, TILE - 8 * f - 4, 2 * TILE - 8 * f - 8)
                shift = lax.rem(shift, TILE)
                strip = fix(f)
                lower = pltpu.roll(strip, 4, 0)
                for b in range(0, TILE, 8):
                    value = cell(f, b)
                    moved = pltpu.roll(turned[b : b + 8, :], shift, 1)
                    edge = jnp.where(col == 0, lane, TILE - 1 - lane) < REACH
                    value = jnp.where(edge, moved, value)
                    if b == 0:
                        value = jnp.where((row == 0) & (sub < REACH), strip, value)
                    if b == TILE - 8:
                        value = jnp.where((row == RT - 1) & (sub >= 8 - REACH), lower, value)
                    packed[s, f, b : b + 8, :] = value

        @pl.when(own & swept)
        def _():
            put(
                lambda f, b: early[row, f, col, PAD + b : PAD + b + 8, :],
                lambda f: fixes[local, f],
            )

        @pl.when(own & jnp.logical_not(swept))
        def _():
            put(
                lambda f, b: late[row, f, col, PAD + b : PAD + b + 8, :],
                lambda f: fixes[local, f],
            )

        @pl.when(foreign)
        def _():
            put(lambda f, b: received[slot, f, b : b + 8, :], lambda f: patches[slot, f])

        @pl.when(entry < 0)
        def _():
            packed[s] = jnp.zeros((3, TILE, TILE), jnp.float32)


def passed_along(block, distance):
    count = lax.axis_size("rows")
    return lax.ppermute(block, "rows", [((i - distance) % count, i) for i in range(count)])


def swapped(block):
    return lax.ppermute(block, "cols", [(0, 1), (1, 0)])


def shards(depth, velocity, bed, slots):
    count = lax.axis_size("rows")
    half = count // 2
    listed = slots[0, 0]
    partner = passed_along(listed, half)
    state, moved = call(
        load_kernel, "load", [VMEM] * 3, [f32(4, CT, DEEP, TILE), f32(4, CT, DEEP, TILE)]
    )(depth, velocity, bed)
    moved, outgoing, early = call(
        send_kernel,
        "send",
        [SMEM, SMEM, VMEM, VMEM],
        [f32(4, CT, DEEP, TILE), f32(MOVED, 3, TILE, TILE), f32(RT, 3, CT, TILE + 2 * PAD, TILE)],
    )(listed, partner, state, moved)
    received = passed_along(outgoing, half)
    (mine,) = call(edge_kernel, "edge", [SMEM, SMEM, VMEM], [f32(5, 32, COLS)])(
        listed, partner, state
    )
    other = swapped(mine)
    (wide,) = call(wide_kernel, "wide", [VMEM, VMEM], [f32(SEAM, 2 * COLS)])(mine, other)
    route = [(2 * r, 2 * r - 1) for r in range(1, count)]
    route += [(2 * r + 1, 2 * r + 2) for r in range(count - 1)]
    came = lax.ppermute(wide, ("rows", "cols"), route)
    near = swapped(came)
    (late,) = call(keep_kernel, "keep", [SMEM, SMEM, VMEM], [f32(RT, 3, CT, TILE + 2 * PAD, TILE)])(
        listed, partner, moved
    )
    flat, tall = (CT + 1, SEAM_DEEP, TILE), (CT, SEAM_DEEP, TILE)
    fixes, sent = call(
        seam_kernel,
        "seam",
        [SMEM, SMEM, VMEM, VMEM, VMEM, VMEM],
        [f32(RT * CT, 3, 8, TILE), f32(MOVED, 3, 8, TILE)],
        [
            pltpu.VMEM((n,) + s, jnp.float32)
            for s in (flat, tall)
            for n in (5, 4, 3)
        ],
    )(listed, partner, mine, other, came, near)
    patches = passed_along(sent, half)
    (packed,) = call(
        pack_kernel,
        "pack",
        [SMEM, SMEM, VMEM, VMEM, VMEM, VMEM, VMEM],
        [f32(SLOTS, 3, TILE, TILE)],
        [pltpu.VMEM((TILE, TILE), jnp.float32)],
    )(listed, partner, early, late, fixes, received, patches)
    return packed[None, None]


def solution(mesh):
    in_specs = (
        P(("groups", "rows"), "cols"),
        P(None, ("groups", "rows"), "cols"),
        P(("groups", "rows"), "cols"),
        P(("groups", "rows"), "cols", None),
    )
    out_specs = P(("groups", "rows"), "cols", None, None, None, None)
    return jax.shard_map(shards, mesh=mesh, in_specs=in_specs, out_specs=out_specs, check_vma=False)
```

time: 74 us -> 62 us (0.84)
  the two profiles are of different devices: /device:TPU:0 before, /device:TPU:1 now
where the time goes in v1:
time: 62 us; the launch traced here: 61.1 us
  Pallas kernels  32.4 us (52%)
  starting transfers between devices  20.7 us (33%)
  waiting for transfers between devices  4.32 us (7%)
  local copies, waits for them, and re-layouts  3.59 us (6%)
    ppermute x3, starting transfers between devices, passed_along(): lax.ppermute(block, 'rows', [((i - distance) % count, i) for i in range(c...  11.3 us
    pallas_call x1, Pallas kernels, shards(): call(load_kernel, 'load', [VMEM] * 3, [f32(4, CT, DEEP, TILE), f32(4, CT,...  10.8 us
    ppermute x1, starting transfers between devices, shards(): came = lax.ppermute(wide, ('rows', 'cols'), route)  8.38 us
    pallas_call x1, Pallas kernels, shards(): call(send_kernel, 'send', [SMEM, SMEM, VMEM, VMEM], [f32(4, CT, DEEP, TIL...  6.49 us
    pallas_call x1, Pallas kernels, shards(): call(keep_kernel, 'keep', [SMEM, SMEM, VMEM], [f32(RT, 3, CT, TILE + 2 *...  6.4 us
    pallas_call x1, Pallas kernels, shards(): call(seam_kernel, 'seam', [SMEM, SMEM, VMEM, VMEM, VMEM, VMEM], [f32(RT *...  5.89 us
    unnamed x8, local copies, waits for them, and re-layouts  3.59 us
    ppermute x2, waiting for transfers between devices, swapped(): return lax.ppermute(block, 'cols', [(0, 1), (1, 0)])  2.26 us
  transfers between devices with their start and end apart: 6, of which 3 were waited for; matrix products, arithmetic and copies ran while one was open for 0% of the time, Pallas kernels for 39%

profile of v1, /device:TPU:1, one launch (start us, length us, event | category | flops | bytes accessed | tf_op | source)
XLA Modules:
  0.0 61.1 jit_solution(3652644336455497006)
XLA Ops:
  0.0 3.1 %collective-permute-start = (s32[3]{0:T(128)}, s32[3]{0:T(128)S(1)}, u32[]{:S(2)}, u32[]{:S(2)}) collective-permute-start(s32[3]{0:T(128)} %bitcast.2), channel_id=1, source_target_pairs={{8,0},{10,2},{12,4},{14,6},{0,8},{2,10},{4,12},{6,14},{9,1},{11,3}... | collective-permute-start | bytes 44 | tf_op jit(solution)/shard_map/ppermute | solution.py:449
  3.1 0.0 copy-start
  3.1 1.0 %copy-done = f32[2,256,256]{2,1,0:T(8,128)S(1)} copy-done((f32[2,256,256]{2,1,0:T(8,128)S(1)}, f32[2,256,256]{2,1,0:T(8,128)}, u32[]{:S(2)}) %copy-start) | copy-done | bytes 524312
  4.2 0.0 copy-start.1
  4.2 0.9 %copy-done.1 = f32[256,256]{1,0:T(8,128)S(1)} copy-done((f32[256,256]{1,0:T(8,128)S(1)}, f32[256,256]{1,0:T(8,128)}, u32[]{:S(2)}) %copy-start.1) | copy-done | bytes 262168
  5.1 0.0 copy-start.2
  5.1 0.9 %copy-done.2 = f32[256,256]{1,0:T(8,128)S(1)} copy-done((f32[256,256]{1,0:T(8,128)S(1)}, f32[256,256]{1,0:T(8,128)}, u32[]{:S(2)}) %copy-start.2) | copy-done | bytes 262168
  6.1 10.8 %load.1 = (f32[4,2,288,128]{3,2,1,0:T(8,128)S(1)}, f32[4,2,288,128]{3,2,1,0:T(8,128)S(1)}) custom-call(f32[256,256]{1,0:T(8,128)S(1)} %copy-done.1, f32[2,256,256]{2,1,0:T(8,128)S(1)} %copy-done, f32[256,256]{1,0:T(8,128)S(1)} %copy-done.2), custom_call_target="tpu_custom_call" | custom-call | tf_op jit(solution)/shard_map/load/pallas_call | solution.py:461
  16.9 0.0 collective-permute-done.partner
  16.9 0.0 copy-start.3
  16.9 0.6 %copy-done.3 = s32[1,1,3]{2,1,0:T(1,128)S(1)} copy-done((s32[1,1,3]{2,1,0:T(1,128)S(1)}, s32[1,1,3]{2,1,0:T(1,128)}, u32[]{:S(2)}) %copy-start.3) | copy-done | bytes 36
  17.5 6.5 %send.1 = (f32[4,2,288,128]{3,2,1,0:T(8,128)S(1)}, f32[2,3,128,128]{3,2,1,0:T(8,128)S(1)}, f32[2,3,2,160,128]{4,3,2,1,0:T(8,128)S(1)}) custom-call(s32[3]{0:T(128)S(1)} %bitcast.3, s32[3]{0:T(128)S(1)} %collective-permute-done.partner, f32[4,2,288,128]{3,2,1,0:T(8,128)S(1)} %get-tuple-element.12.state, f32[4,2,288,128]{3,2,1,0:T(8,128)S(1)} %get-tuple-element.13.guess), custom_call_target="tpu_custom_call" | custom-call | tf_op jit(solution)/shard_map/send/pallas_call | solution.py:464
  24.0 0.1 collective-permute-start.4
  24.1 0.7 %edge.1.mine = f32[5,32,256]{2,1,0:T(8,128)S(1)} custom-call(s32[3]{0:T(128)S(1)} %bitcast.4, s32[3]{0:T(128)S(1)} %collective-permute-done.partner, f32[4,2,288,128]{3,2,1,0:T(8,128)S(1)} %get-tuple-element.12.state), custom_call_target="tpu_custom_call" | custom-call | tf_op jit(solution)/shard_map/edge/pallas_call | solution.py:471
  24.8 1.0 %collective-permute-start.1 = (f32[5,32,256]{2,1,0:T(8,128)S(1)}, f32[5,32,256]{2,1,0:T(8,128)S(1)}, u32[]{:S(2)}, u32[]{:S(2)}) collective-permute-start(f32[5,32,256]{2,1,0:T(8,128)S(1)} %edge.1.mine), channel_id=1, source_target_pairs={{0,1},{1,0},{2,3},{3,2},{4,5},{5,4},{6,7},{7,6},{8,9},{9,8},{10,11... | collective-permute-start | bytes 491528 | tf_op jit(solution)/shard_map/ppermute | solution.py:453
  25.9 1.0 %collective-permute-done.1.other = f32[5,32,256]{2,1,0:T(8,128)S(1)} collective-permute-done((f32[5,32,256]{2,1,0:T(8,128)S(1)}, f32[5,32,256]{2,1,0:T(8,128)S(1)}, u32[]{:S(2)}, u32[]{:S(2)}) %collective-permute-start.1) | collective-permute-done | bytes 163872 | tf_op jit(solution)/shard_map/ppermute | solution.py:453
  26.9 8.4 %collective-permute-start.2 = (f32[24,512]{1,0:T(8,128)S(1)}, f32[24,512]{1,0:T(8,128)S(1)}, u32[]{:S(2)}, u32[]{:S(2)}) collective-permute-start(f32[24,512]{1,0:T(8,128)S(1)} %wide.1), channel_id=1, source_target_pairs={{2,1},{4,3},{6,5},{8,7},{10,9},{12,11},{14,13},{1,2},{3,4},{5,6},{... | collective-permute-start | bytes 147464 | tf_op jit(solution)/shard_map/ppermute | solution.py:478
  35.3 2.1 %collective-permute-done.2.came = f32[24,512]{1,0:T(8,128)S(1)} collective-permute-done((f32[24,512]{1,0:T(8,128)S(1)}, f32[24,512]{1,0:T(8,128)S(1)}, u32[]{:S(2)}, u32[]{:S(2)}) %collective-permute-start.2) | collective-permute-done | bytes 49184 | tf_op jit(solution)/shard_map/ppermute | solution.py:478
  37.4 0.0 collective-permute-start.3
  37.4 1.2 %collective-permute-done.3.near = f32[24,512]{1,0:T(8,128)S(1)} collective-permute-done((f32[24,512]{1,0:T(8,128)S(1)}, f32[24,512]{1,0:T(8,128)S(1)}, u32[]{:S(2)}, u32[]{:S(2)}) %collective-permute-start.3) | collective-permute-done | bytes 49184 | tf_op jit(solution)/shard_map/ppermute | solution.py:453
  38.6 5.9 %seam.1 = (f32[4,3,8,128]{3,2,1,0:T(8,128)S(1)}, f32[2,3,8,128]{3,2,1,0:T(8,128)S(1)}) custom-call(s32[3]{0:T(128)S(1)} %bitcast.5, s32[3]{0:T(128)S(1)} %collective-permute-done.partner, f32[5,32,256]{2,1,0:T(8,128)S(1)} %edge.1.mine, f32[5,32,256]{2,1,0:T(8,128)S(1)} %collective-permute-done.1.other, f32[24,512]{1,0:T(8,128)S(1)} %collective-permute-done.2.came, ...), custom_call_target="tpu_custom_call" | custom-call | tf_op jit(solution)/shard_map/seam/pallas_call | solution.py:484
  44.5 8.1 %collective-permute-start.5 = (f32[2,3,8,128]{3,2,1,0:T(8,128)S(1)}, f32[2,3,8,128]{3,2,1,0:T(8,128)S(1)}, u32[]{:S(2)}, u32[]{:S(2)}) collective-permute-start(f32[2,3,8,128]{3,2,1,0:T(8,128)S(1)} %get-tuple-element.18), channel_id=1, source_target_pairs={{8,0},{10,2},{12,4},{14,6},{0,8},{2,10},{4,12},{6,14},{9,1},{11,3}... | collective-permute-start | bytes 73736 | tf_op jit(solution)/shard_map/ppermute | solution.py:449
  52.6 6.4 %keep.1.late = f32[2,3,2,160,128]{4,3,2,1,0:T(8,128)S(1)} custom-call(s32[3]{0:T(128)S(1)} %bitcast.6, s32[3]{0:T(128)S(1)} %collective-permute-done.partner, f32[4,2,288,128]{3,2,1,0:T(8,128)S(1)} %get-tuple-element.15.moved), custom_call_target="tpu_custom_call" | custom-call | tf_op jit(solution)/shard_map/keep/pallas_call | solution.py:480
  59.0 0.0 collective-permute-done.5.patches
  59.0 0.0 collective-permute-done.4.received
  59.0 2.1 %pack.1 = f32[3,3,128,128]{3,2,1,0:T(8,128)} custom-call(s32[3]{0:T(128)S(1)} %bitcast.7, s32[3]{0:T(128)S(1)} %collective-permute-done.partner, f32[2,3,2,160,128]{4,3,2,1,0:T(8,128)S(1)} %get-tuple-element.14.early, f32[2,3,2,160,128]{4,3,2,1,0:T(8,128)S(1)} %keep.1.late, f32[4,3,8,128]{3,2,1,0:T(8,128)S(1)} %get-tuple-element.16.fixes, ...), custom_call_target="tpu_custom_call" | custom-call | tf_op jit(solution)/shard_map/pack/pallas_call | solution.py:496
  (1 shorter events, 0.0 us)
Async XLA Ops:
  0.0 16.9 %collective-permute-start = (s32[3]{0:T(128)}, s32[3]{0:T(128)S(1)}, u32[]{:S(2)}, u32[]{:S(2)}) collective-permute-start(s32[3]{0:T(128)} %bitcast.2), channel_id=1, source_target_pairs={{8,0},{10,2},{12,4},{14,6},{0,8},{2,10},{4,12},{6,14},{9,1},{11,3}... | collective-permute-start | bytes 44 | tf_op jit(solution)/shard_map/ppermute | solution.py:449
  3.1 1.0 %copy-start = (f32[2,256,256]{2,1,0:T(8,128)S(1)}, f32[2,256,256]{2,1,0:T(8,128)}, u32[]{:S(2)}) copy-start(f32[2,256,256]{2,1,0:T(8,128)} %velocity.1) | copy-start | bytes 1572868
  4.2 0.9 %copy-start.1 = (f32[256,256]{1,0:T(8,128)S(1)}, f32[256,256]{1,0:T(8,128)}, u32[]{:S(2)}) copy-start(f32[256,256]{1,0:T(8,128)} %depth.1) | copy-start | bytes 786436
  5.1 0.9 %copy-start.2 = (f32[256,256]{1,0:T(8,128)S(1)}, f32[256,256]{1,0:T(8,128)}, u32[]{:S(2)}) copy-start(f32[256,256]{1,0:T(8,128)} %bed.1) | copy-start | bytes 786436
  16.9 0.7 %copy-start.3 = (s32[1,1,3]{2,1,0:T(1,128)S(1)}, s32[1,1,3]{2,1,0:T(1,128)}, u32[]{:S(2)}) copy-start(s32[1,1,3]{2,1,0:T(1,128)} %param.7) | copy-start | bytes 40
  24.0 35.0 %collective-permute-start.4 = (f32[2,3,128,128]{3,2,1,0:T(8,128)S(1)}, f32[2,3,128,128]{3,2,1,0:T(8,128)S(1)}, u32[]{:S(2)}, u32[]{:S(2)}) collective-permute-start(f32[2,3,128,128]{3,2,1,0:T(8,128)S(1)} %get-tuple-element.17), channel_id=1, source_target_pairs={{8,0},{10,2},{12,4},{14,6},{0,8},{2,10},{4,12},{6,14},{9,1},{11,3}... | collective-permute-start | bytes 1179656 | tf_op jit(solution)/shard_map/ppermute | solution.py:449
  24.8 2.0 %collective-permute-start.1 = (f32[5,32,256]{2,1,0:T(8,128)S(1)}, f32[5,32,256]{2,1,0:T(8,128)S(1)}, u32[]{:S(2)}, u32[]{:S(2)}) collective-permute-start(f32[5,32,256]{2,1,0:T(8,128)S(1)} %edge.1.mine), channel_id=1, source_target_pairs={{0,1},{1,0},{2,3},{3,2},{4,5},{5,4},{6,7},{7,6},{8,9},{9,8},{10,11... | collective-permute-start | bytes 491528 | tf_op jit(solution)/shard_map/ppermute | solution.py:453
  26.9 10.4 %collective-permute-start.2 = (f32[24,512]{1,0:T(8,128)S(1)}, f32[24,512]{1,0:T(8,128)S(1)}, u32[]{:S(2)}, u32[]{:S(2)}) collective-permute-start(f32[24,512]{1,0:T(8,128)S(1)} %wide.1), channel_id=1, source_target_pairs={{2,1},{4,3},{6,5},{8,7},{10,9},{12,11},{14,13},{1,2},{3,4},{5,6},{... | collective-permute-start | bytes 147464 | tf_op jit(solution)/shard_map/ppermute | solution.py:478
  37.4 1.2 %collective-permute-start.3 = (f32[24,512]{1,0:T(8,128)S(1)}, f32[24,512]{1,0:T(8,128)S(1)}, u32[]{:S(2)}, u32[]{:S(2)}) collective-permute-start(f32[24,512]{1,0:T(8,128)S(1)} %collective-permute-done.2.came), channel_id=1, source_target_pairs={{0,1},{1,0},{2,3},{3,2},{4,5},{5,4},{6,7},{7,6},{8,9},{9,8},{10,11... | collective-permute-start | bytes 147464 | tf_op jit(solution)/shard_map/ppermute | solution.py:453
  44.5 14.5 %collective-permute-start.5 = (f32[2,3,8,128]{3,2,1,0:T(8,128)S(1)}, f32[2,3,8,128]{3,2,1,0:T(8,128)S(1)}, u32[]{:S(2)}, u32[]{:S(2)}) collective-permute-start(f32[2,3,8,128]{3,2,1,0:T(8,128)S(1)} %get-tuple-element.18), channel_id=1, source_target_pairs={{8,0},{10,2},{12,4},{14,6},{0,8},{2,10},{4,12},{6,14},{9,1},{11,3}... | collective-permute-start | bytes 73736 | tf_op jit(solution)/shard_map/ppermute | solution.py:449

commit v2 on v1

v2 whole, which is shorter than its diff:
```python
import jax
import jax.numpy as jnp
from jax import lax
from jax.experimental import pallas as pl
from jax.experimental.pallas import tpu as pltpu
from jax.sharding import PartitionSpec as P


TILE = 128
RT = 2
CT = 2
SLOTS = 3
MOVED = RT * CT // 2
ROWS = RT * TILE
COLS = CT * TILE
PAD = 16
SEAM = 40
SEAM_DEEP = SEAM + 2 * PAD
SPAN = TILE + 2 * PAD
PART = TILE // 2
REACH = 4
UNROLL_PART = 2
UNROLL_FULL = 3
UNROLL_SEAM = 1

GRAVITY = 9.81
TIME_STEP = 0.04
DRY_DEPTH = 0.05
SPEED_FLOOR = 0.5
ROOT_GRAVITY = GRAVITY**0.5
TINY = 1.2e-38

VMEM = pl.BlockSpec(memory_space=pltpu.VMEM)
HBM = pl.BlockSpec(memory_space=pltpu.HBM)
SMEM = pl.BlockSpec(memory_space=pltpu.SMEM)


def f32(*shape):
    return jax.ShapeDtypeStruct(shape, jnp.float32)


def call(kernel, ins, outs, scratch=(), room=20 * 2**20):
    return pl.pallas_call(
        kernel,
        in_specs=list(ins),
        out_specs=tuple(VMEM for _ in outs),
        out_shape=tuple(outs),
        scratch_shapes=list(scratch),
        compiler_params=pltpu.CompilerParams(vmem_limit_bytes=room),
    )


def limited(down, up):
    return 0.5 * jnp.maximum(jnp.minimum(down, jnp.maximum(up, 0.0)), jnp.minimum(up, 0.0))


def speeds(water, normal, across):
    square = water * water
    factor = (water + water) / (square + jnp.maximum(square, DRY_DEPTH * DRY_DEPTH))
    return factor * normal, factor * across


def wave_speed(level):
    return (ROOT_GRAVITY * level) * lax.rsqrt(jnp.maximum(level, TINY))


def face_flux(left, right):
    water_l, speed_l, drift_l, ground_l = left
    water_r, speed_r, drift_r, ground_r = right
    top = jnp.maximum(ground_l, ground_r)
    level_l = jnp.maximum(water_l + (ground_l - top), 0.0)
    level_r = jnp.maximum(water_r + (ground_r - top), 0.0)
    wave_l = wave_speed(level_l)
    wave_r = wave_speed(level_r)
    lower = jnp.minimum(jnp.minimum(speed_l - wave_l, speed_r - wave_r), 0.0)
    upper = jnp.maximum(jnp.maximum(speed_l + wave_l, speed_r + wave_r), 0.0)
    inverse = 1.0 / jnp.maximum(upper - lower, SPEED_FLOOR)
    up = upper * inverse
    low = lower * inverse
    both = upper * low
    part_l = level_l * (up * speed_l - both)
    part_r = level_r * (both - low * speed_r)
    press_l = (0.5 * GRAVITY) * (level_l * level_l)
    press_r = (0.5 * GRAVITY) * (level_r * level_r)
    mass = part_l + part_r
    push = part_l * speed_l + part_r * speed_r + up * press_l - low * press_r
    side = part_l * drift_l + part_r * drift_r
    return mass, push - press_l, push - press_r, side


def sweep(src, ground, dst, width, steps, row_start, lane_flow, row_flow, unroll, flush):
    sub = lax.broadcasted_iota(jnp.int32, (8, 128), 0)
    cols = range(width)

    def step(i, carry):
        row = row_start + pl.multiple_of(i * 8, 8)

        def read(f, w, offset):
            held = src if f < 3 else ground
            return held[f, w, pl.ds(row + offset, 8), :]

        now = []
        for w in cols:
            x = [read(f, w, 0) for f in range(4)]
            low, high, half = [], [], []
            for f in (0, lane_flow, row_flow, 3):
                down = x[f] - pltpu.roll(x[f], 1, 1)
                hs = limited(down, pltpu.roll(down, TILE - 1, 1))
                low.append(x[f] - hs)
                high.append(x[f] + hs)
                half.append(hs)
            fast = speeds(high[0], high[1], high[2])
            slow = speeds(low[0], low[1], low[2])
            left = [pltpu.roll(v, 1, 1) for v in (high[0], fast[0], fast[1], high[3])]
            mass, push_l, push_r, side = face_flux(left, (low[0], slow[0], slow[1], low[3]))
            weight = (2.0 * GRAVITY) * x[0]
            gain_water = mass - pltpu.roll(mass, TILE - 1, 1)
            gain_lane = push_r - pltpu.roll(push_l, TILE - 1, 1) - weight * (half[0] + half[3])
            gain_row = side - pltpu.roll(side, TILE - 1, 1)
            low, high, half = [], [], []
            for f in (0, row_flow, lane_flow, 3):
                hs = limited(x[f] - read(f, w, -1), read(f, w, 1) - x[f])
                low.append(x[f] - hs)
                high.append(x[f] + hs)
                half.append(hs)
            fast = speeds(high[0], high[1], high[2])
            slow = speeds(low[0], low[1], low[2])
            old_high, old_flux, old_gain = carry[w]
            high_now = tuple(pltpu.roll(v, 1, 0) for v in (high[0], fast[0], fast[1], high[3]))
            left = [jnp.where(sub == 0, o, n) for o, n in zip(old_high, high_now)]
            mass, push_l, push_r, side = face_flux(left, (low[0], slow[0], slow[1], low[3]))
            gain = (
                gain_water + mass,
                gain_lane + side,
                gain_row + push_r - weight * (half[0] + half[3]),
            )
            flux_now = tuple(pltpu.roll(v, 7, 0) for v in (mass, side, push_l))
            for f, g, o, n in zip((0, lane_flow, row_flow), old_gain, old_flux, flux_now):
                dst[f, w, pl.ds(row - 8, 8), :] = read(f, w, -8) + TIME_STEP * (
                    g - jnp.where(sub == 7, n, o)
                )
            now.append((high_now, flux_now, gain))
        return tuple(now)

    zero = jnp.zeros((8, 128), jnp.float32)
    start = tuple(((zero,) * 4, (zero,) * 3, (zero,) * 3) for _ in cols)
    carry = lax.fori_loop(0, steps, step, start, unroll=unroll)
    if flush:
        row = row_start + 8 * (steps - 1)
        for w in cols:
            _, old_flux, old_gain = carry[w]
            for f, g, o in zip((0, lane_flow, row_flow), old_gain, old_flux):
                dst[f, w, row : row + 8, :] = src[f, w, row : row + 8, :] + TIME_STEP * (g - o)


def load_kernel(depth, velocity, bed, state, water, speed, ground, sems):
    copies = [
        pltpu.make_async_copy(depth, water, sems.at[0]),
        pltpu.make_async_copy(velocity, speed, sems.at[1]),
        pltpu.make_async_copy(bed, ground, sems.at[2]),
    ]
    for copy in copies:
        copy.start()
    for copy in copies:
        copy.wait()
    for w in range(CT):
        cols = slice(w * TILE, (w + 1) * TILE)
        for r in range(0, ROWS, 8):
            rows = slice(r, r + 8)
            here = water[rows, cols]
            state[0, w, rows, :] = here
            state[1, w, rows, :] = here * speed[0, rows, cols]
            state[2, w, rows, :] = here * speed[1, rows, cols]
            state[3, w, rows, :] = ground[rows, cols]


class Lists:
    def __init__(self, listed, partner):
        self.rows = lax.axis_index("rows")
        self.cols = lax.axis_index("cols")
        self.span = CT * lax.axis_size("cols")
        self.ids = [
            (self.rows * RT + t // CT) * self.span + self.cols * CT + t % CT for t in range(RT * CT)
        ]
        self.listed = [listed[k] for k in range(SLOTS)]
        self.partner = [partner[k] for k in range(SLOTS)]

    def inside(self, entry):
        found = [entry == i for i in self.ids]
        any_found = found[0]
        local = jnp.int32(0)
        for t in range(1, RT * CT):
            any_found = any_found | found[t]
            local = jnp.where(found[t], jnp.int32(t), local)
        return any_found, local

    def active(self, t):
        hit = self.listed[0] == self.ids[t]
        for entry in self.listed[1:] + self.partner:
            hit = hit | (entry == self.ids[t])
        return hit

    def outgoing(self):
        used = [jnp.bool_(False)] * MOVED
        tile = [jnp.int32(0)] * MOVED
        rank = jnp.int32(0)
        for entry in self.partner:
            own, local = self.inside(entry)
            for k in range(MOVED):
                take = own & (rank == k)
                used[k] = used[k] | take
                tile[k] = jnp.where(take, local, tile[k])
            rank = rank + own.astype(jnp.int32)
        return used, tile

    def kept(self):
        used = [jnp.bool_(False)] * MOVED
        tile = [jnp.int32(0)] * MOVED
        rank = jnp.int32(0)
        for entry in self.listed:
            own, local = self.inside(entry)
            for k in range(MOVED):
                take = own & (rank == k)
                used[k] = used[k] | take
                tile[k] = jnp.where(take, local, tile[k])
            rank = rank + own.astype(jnp.int32)
        return used, tile


def edge_kernel(listed, partner, state, strips, inner):
    lists = Lists(listed, partner)
    lane = lax.broadcasted_iota(jnp.int32, (TILE, TILE), 1)
    for f in range(4):
        for w in range(CT):
            cols = slice(w * TILE, (w + 1) * TILE)
            strips[f, 0:8, cols] = state[f, w, ROWS - 8 : ROWS, :]
            strips[f, 8:16, cols] = state[f, w, 0:8, :]
        for r in range(RT):
            rows = slice(r * TILE, (r + 1) * TILE)
            cols = slice(r * TILE, (r + 1) * TILE)
            one, two = state[f, 0, rows, :], state[f, CT - 1, rows, :]
            turned = jnp.where(lane < TILE // 2, one, two).T
            strips[f, 16:24, cols] = turned[TILE - 8 :, :]
            strips[f, 24:32, cols] = turned[:8, :]
            turned = jnp.where(lane < TILE // 2, two, one).T
            inner[f, 0:8, cols] = turned[TILE - 8 :, :]
            inner[f, 8:16, cols] = turned[:8, :]
    flags = [jnp.where(lists.active(t), 1.0, 0.0) for t in range(RT * CT)]

    def full(t):
        return jnp.full((8, TILE), flags[t], jnp.float32)

    for w in range(CT):
        cols = slice(w * TILE, (w + 1) * TILE)
        strips[4, 0:8, cols] = full((RT - 1) * CT + w)
        strips[4, 8:16, cols] = full(w)
    for r in range(RT):
        cols = slice(r * TILE, (r + 1) * TILE)
        strips[4, 16:24, cols] = full(r * CT + CT - 1)
        strips[4, 24:32, cols] = full(r * CT)
        inner[4, 0:8, cols] = full(r * CT)
        inner[4, 8:16, cols] = full(r * CT + CT - 1)


def wide_kernel(mine, other, out):
    is_left = lax.axis_index("cols") == 0
    for f in range(5):
        own = jnp.where(is_left, mine[f, 8:12, :], mine[f, 4:8, :])
        near = jnp.where(is_left, other[f, 8:12, :], other[f, 4:8, :])
        out[4 * f : 4 * f + 4, 0:COLS] = jnp.where(is_left, own, near)
        out[4 * f : 4 * f + 4, COLS : 2 * COLS] = jnp.where(is_left, near, own)
    out[20:24, :] = jnp.zeros((4, 2 * COLS), jnp.float32)


def halo_rows(came, near, f, upper, is_left):
    rows = slice(4 * f, 4 * f + 4)
    return jnp.where(is_left == upper, came[rows, :], near[rows, :])


def gather_pair(tile, state, mine, came, near, start):
    is_left = lax.axis_index("cols") == 0
    blank = jnp.zeros((4, TILE), jnp.float32)
    for k in range(MOVED):
        r, c = tile[k] // CT, tile[k] % CT
        base = pl.multiple_of(r * TILE, TILE)
        for f in range(4):
            start[f, k, PAD : PAD + TILE, :] = state[f, c, pl.ds(base, TILE), :]
        for f in range(5):
            above = halo_rows(came, near, f, True, is_left)
            below = halo_rows(came, near, f, False, is_left)
            ends = []
            for halo in (above, below):
                pieces = [halo[:, q * TILE : (q + 1) * TILE] for q in range(2 * CT)]
                first = jnp.where(is_left, pieces[0], pieces[2])
                second = jnp.where(is_left, pieces[1], pieces[3])
                ends.append(jnp.where(c == 0, first, second))

            @pl.when(r == 0)
            def _(f=f, k=k, c=c, ends=ends):
                start[f, k, PAD - 8 : PAD - 4, :] = blank
                start[f, k, PAD - 4 : PAD, :] = ends[0]
                if f < 4:
                    start[f, k, PAD + TILE : PAD + TILE + 8, :] = state[f, c, TILE : TILE + 8, :]
                else:
                    flag = jnp.where(c == 0, mine[4, 0:8, 0:TILE], mine[4, 0:8, TILE : 2 * TILE])
                    start[f, k, PAD + TILE : PAD + TILE + 8, :] = flag

            @pl.when(r == RT - 1)
            def _(f=f, k=k, c=c, ends=ends):
                start[f, k, PAD + TILE : PAD + TILE + 4, :] = ends[1]
                start[f, k, PAD + TILE + 4 : PAD + TILE + 8, :] = blank
                if f < 4:
                    start[f, k, PAD - 8 : PAD, :] = state[f, c, TILE - 8 : TILE, :]
                else:
                    flag = jnp.where(c == 0, mine[4, 8:16, 0:TILE], mine[4, 8:16, TILE : 2 * TILE])
                    start[f, k, PAD - 8 : PAD, :] = flag


def still(dst, src, width, rows):
    for w in range(width):
        alive = src[4, w, rows, :] > 0.5
        for f in range(3):
            dst[f, w, rows, :] = jnp.where(alive, dst[f, w, rows, :], src[f, w, rows, :])


def advance_pair(start, middle, end, first, last, unroll):
    steps = (last - first) // 8 + 2
    row = PAD + first - 8
    sweep(start, start, middle, MOVED, steps, row, 1, 2, unroll, True)
    if first == 0:
        still(middle, start, MOVED, slice(PAD - 8, PAD))
    if last == TILE:
        still(middle, start, MOVED, slice(PAD + TILE, PAD + TILE + 8))
    sweep(middle, start, end, MOVED, steps, row, 1, 2, unroll, False)


def overlay(cell, fix, board, store):
    lane = lax.broadcasted_iota(jnp.int32, (8, TILE), 1)
    for f in range(3):
        board[8 * f : 8 * f + 8, :] = fix(f)
    turned = board[...].T
    for f in range(3):
        for b in range(0, TILE, 8):
            strip = turned[b : b + 8, :]
            left = pltpu.roll(strip, (TILE - 8 * f) % TILE, 1)
            right = pltpu.roll(strip, TILE - 8 - 8 * f, 1)
            value = jnp.where(lane < REACH, left, cell(f, b))
            store(f, b, jnp.where(lane >= TILE - REACH, right, value))


def upper_kernel(listed, partner, state, mine, came, near, start, out, middle, end):
    _, tile = Lists(listed, partner).outgoing()
    gather_pair(tile, state, mine, came, near, start)
    advance_pair(start, middle, end, 0, PART, UNROLL_PART)
    for k in range(MOVED):
        for f in range(3):
            out[k, f] = end[f, k, PAD : PAD + PART, :]


def lower_kernel(listed, partner, start, fixes, out, middle, end):
    _, tile = Lists(listed, partner).outgoing()
    advance_pair(start, middle, end, PART, TILE, UNROLL_PART)
    for k in range(MOVED):
        for f in range(3):
            out[k, f, 0:PART, :] = end[f, k, PAD + PART : PAD + TILE, :]
            out[k, f, PART : PART + 8, :] = fixes[tile[k], f]


def keep_kernel(listed, partner, state, mine, came, near, fixes, after, out, start, middle, end, board):
    del after
    used, tile = Lists(listed, partner).kept()

    @pl.when(used[0])
    def _():
        gather_pair(tile, state, mine, came, near, start)
        advance_pair(start, middle, end, 0, TILE, UNROLL_FULL)
        board[...] = jnp.zeros_like(board)
        for k in range(MOVED):

            def store(f, b, value, k=k):
                out[k, f, b : b + 8, :] = value

            overlay(
                lambda f, b, k=k: end[f, k, PAD + b : PAD + b + 8, :],
                lambda f, k=k: fixes[tile[k], f],
                board,
                store,
            )


def seam_kernel(mine, other, inner, came, near, after, fixes, start, middle, end, one, two, side, board):
    del after
    is_left = lax.axis_index("cols") == 0
    lane = lax.broadcasted_iota(jnp.int32, (8, TILE), 1)
    for f in range(5):
        for w in range(CT):
            cols = slice(w * TILE, (w + 1) * TILE)
            start[f, w, PAD : PAD + 8, :] = mine[f, 16:24, cols]
            start[f, w, PAD + 8 : PAD + 12, :] = jnp.where(is_left, other[f, 24:28, cols], 0.0)
            start[f, w, PAD + 12 : PAD + 16, :] = jnp.where(is_left, 0.0, other[f, 20:24, cols])
            start[f, w, PAD + 16 : PAD + 24, :] = mine[f, 24:32, cols]
            start[f, w, PAD + 24 : PAD + 40, :] = inner[f, :, cols]
        for place, upper in ((0, False), (4, True)):
            halo = halo_rows(came, near, f, upper, is_left)
            pieces = [halo[:, q * TILE : (q + 1) * TILE] for q in range(2 * CT)]
            rows = slice(8 * f + place, 8 * f + place + 4)
            one[rows, :] = jnp.where(is_left, pieces[0], pieces[2])
            two[rows, :] = jnp.where(is_left, pieces[1], pieces[3])
            side[rows, :] = jnp.where(is_left, pieces[2], pieces[1])
    board[...] = jnp.zeros_like(board)
    for b in range(0, 40, 8):
        rows = slice(b, b + 8)
        first, second, beside = one[rows, :], two[rows, :], side[rows, :]
        value = jnp.where(lane < 8, pltpu.roll(second, 8, 1), 0.0)
        value = jnp.where((lane >= 8) & (lane < 12) & is_left, pltpu.roll(beside, 8, 1), value)
        far = jnp.logical_not(is_left)
        value = jnp.where((lane >= 12) & (lane < 16) & far, pltpu.roll(beside, 16, 1), value)
        value = jnp.where((lane >= 16) & (lane < 24), pltpu.roll(first, 16, 1), value)
        value = jnp.where((lane >= 24) & (lane < 32), pltpu.roll(first, 32, 1), value)
        board[rows, :] = jnp.where((lane >= 32) & (lane < 40), pltpu.roll(second, 32, 1), value)
    turned = board[...].T
    for f in range(5):
        for b in range(0, SEAM, 8):
            rows = slice(PAD + b, PAD + b + 8)
            first, second = start[f, 0, rows, :], start[f, 1, rows, :]
            ends = pltpu.roll(turned[b : b + 8, :], (8 - 8 * f) % TILE, 1)
            value = jnp.where(lane < 8, pltpu.roll(second, 8, 1), 0.0)
            value = jnp.where((lane >= 8) & (lane < 16), ends, value)
            value = jnp.where((lane >= 16) & (lane < 24), pltpu.roll(first, 16, 1), value)
            value = jnp.where((lane >= 24) & (lane < 32), pltpu.roll(first, 32, 1), value)
            start[f, CT, rows, :] = jnp.where(
                (lane >= 32) & (lane < 40), pltpu.roll(second, 32, 1), value
            )
    width = CT + 1
    sweep(start, start, middle, width, SEAM // 8, PAD, 2, 1, UNROLL_SEAM, True)
    still(middle, start, width, slice(PAD, PAD + SEAM))
    sweep(middle, start, end, width, SEAM // 8, PAD, 2, 1, UNROLL_SEAM, True)
    lane = lax.broadcasted_iota(jnp.int32, (4, TILE), 1)
    for t in range(RT * CT):
        r, c = t // CT, t % CT
        for place, row in ((0, 16 if c == 0 else 32), (4, 28 if c == 0 else 4)):
            rows = slice(PAD + row, PAD + row + 4)
            for f in range(3):
                ends = end[f, CT, rows, :]
                low = pltpu.roll(ends, 112 if r == 0 else 96, 1)
                high = pltpu.roll(ends, 96 if r == 0 else 120, 1)
                value = jnp.where(lane < REACH, low, end[f, r, rows, :])
                fixes[t, f, place : place + 4, :] = jnp.where(lane >= TILE - REACH, high, value)


def pack_kernel(listed, partner, kept, upper, lower, packed, board):
    lists = Lists(listed, partner)
    board[...] = jnp.zeros_like(board)
    far = jnp.int32(0)
    near = jnp.int32(0)
    for s in range(SLOTS):
        entry = lists.listed[s]
        own, _ = lists.inside(entry)
        foreign = (entry >= 0) & jnp.logical_not(own)
        here = jnp.minimum(near, MOVED - 1)
        there = jnp.minimum(far, MOVED - 1)
        near = near + own.astype(jnp.int32)
        far = far + foreign.astype(jnp.int32)

        @pl.when(own)
        def _(s=s, here=here):
            packed[s] = kept[here]

        @pl.when(foreign)
        def _(s=s, there=there):
            def cell(f, b):
                if b < PART:
                    return upper[there, f, b : b + 8, :]
                return lower[there, f, b - PART : b - PART + 8, :]

            def store(f, b, value):
                packed[s, f, b : b + 8, :] = value

            overlay(cell, lambda f: lower[there, f, PART : PART + 8, :], board, store)

        @pl.when(entry < 0)
        def _(s=s):
            packed[s] = jnp.zeros((3, TILE, TILE), jnp.float32)


def passed_along(block, distance):
    count = lax.axis_size("rows")
    return lax.ppermute(block, "rows", [((i - distance) % count, i) for i in range(count)])


def swapped(block):
    return lax.ppermute(block, "cols", [(0, 1), (1, 0)])


def scratch(*shape):
    return pltpu.VMEM(shape, jnp.float32)


def shards(depth, velocity, bed, slots):
    count = lax.axis_size("rows")
    half = count // 2
    listed = slots[0, 0]
    partner = passed_along(listed, half)
    (state,) = call(
        load_kernel,
        [HBM] * 3,
        [f32(4, CT, ROWS, TILE)],
        [
            scratch(ROWS, COLS),
            scratch(2, ROWS, COLS),
            scratch(ROWS, COLS),
            pltpu.SemaphoreType.DMA((3,)),
        ],
    )(depth, velocity, bed)
    mine, inner = call(
        edge_kernel, [SMEM, SMEM, VMEM], [f32(5, 32, COLS), f32(5, 16, COLS)]
    )(listed, partner, state)
    other = swapped(mine)
    (wide,) = call(wide_kernel, [VMEM, VMEM], [f32(24, 2 * COLS)])(mine, other)
    route = [(2 * r, 2 * r - 1) for r in range(1, count)]
    route += [(2 * r + 1, 2 * r + 2) for r in range(count - 1)]
    came = lax.ppermute(wide, ("rows", "cols"), route)
    near = swapped(came)
    pair = [scratch(3, MOVED, SPAN, TILE)] * 2
    start, upper = call(
        upper_kernel,
        [SMEM, SMEM] + [VMEM] * 4,
        [f32(5, MOVED, SPAN, TILE), f32(MOVED, 3, PART, TILE)],
        pair,
    )(listed, partner, state, mine, came, near)
    far_upper = passed_along(upper, half)
    (fixes,) = call(
        seam_kernel,
        [VMEM] * 5 + [pl.BlockSpec(memory_space=pl.ANY)],
        [f32(RT * CT, 3, 8, TILE)],
        [scratch(5, CT + 1, SEAM_DEEP, TILE)]
        + [scratch(3, CT + 1, SEAM_DEEP, TILE)] * 2
        + [scratch(40, TILE)] * 3
        + [scratch(TILE, TILE)],
    )(mine, other, inner, came, near, upper)
    (lower,) = call(
        lower_kernel, [SMEM, SMEM, VMEM, VMEM], [f32(MOVED, 3, PART + 8, TILE)], pair
    )(listed, partner, start, fixes)
    far_lower = passed_along(lower, half)
    (kept,) = call(
        keep_kernel,
        [SMEM, SMEM] + [VMEM] * 5 + [pl.BlockSpec(memory_space=pl.ANY)],
        [f32(MOVED, 3, TILE, TILE)],
        [scratch(5, MOVED, SPAN, TILE)] + pair + [scratch(TILE, TILE)],
    )(listed, partner, state, mine, came, near, fixes, lower)
    (packed,) = call(
        pack_kernel, [SMEM, SMEM] + [VMEM] * 3, [f32(SLOTS, 3, TILE, TILE)], [scratch(TILE, TILE)]
    )(listed, partner, kept, far_upper, far_lower)
    return packed[None, None]


def solution(mesh):
    in_specs = (
        P(("groups", "rows"), "cols"),
        P(None, ("groups", "rows"), "cols"),
        P(("groups", "rows"), "cols"),
        P(("groups", "rows"), "cols", None),
    )
    out_specs = P(("groups", "rows"), "cols", None, None, None, None)

    return jax.shard_map(shards, mesh=mesh, in_specs=in_specs, out_specs=out_specs, check_vma=False)
```

time: 62 us -> 52 us (0.84)
  the two profiles are of different devices: /device:TPU:1 before, /device:TPU:0 now
where the time goes in v2:
time: 52 us; the launch traced here: 51.8 us
  Pallas kernels  19.9 us (38%)
  waiting for transfers between devices  15.6 us (30%)
  starting transfers between devices  12.7 us (24%)
  local copies, waits for them, and re-layouts  3.59 us (7%)
    ppermute x3, waiting for transfers between devices, passed_along(): lax.ppermute(block, 'rows', [((i - distance) % count, i) for i in range(c...  13.3 us
    ppermute x3, starting transfers between devices, passed_along(): lax.ppermute(block, 'rows', [((i - distance) % count, i) for i in range(c...  7.05 us
    pallas_call x1, Pallas kernels, shards(): call(keep_kernel, [SMEM, SMEM] + [VMEM] * 5 + [pl.BlockSpec(memory_space=...  5.52 us
    ppermute x2, starting transfers between devices, swapped(): return lax.ppermute(block, 'cols', [(0, 1), (1, 0)])  4.94 us
    pallas_call x1, Pallas kernels, shards(): call(upper_kernel, [SMEM, SMEM] + [VMEM] * 4, [f32(5, MOVED, SPAN, TILE),...  4.05 us
    pallas_call x1, Pallas kernels, shards(): call(lower_kernel, [SMEM, SMEM, VMEM, VMEM], [f32(MOVED, 3, PART + 8, TIL...  3.93 us
    pallas_call x1, Pallas kernels, shards(): call(seam_kernel, [VMEM] * 5 + [pl.BlockSpec(memory_space=pl.ANY)], [f32(...  3.72 us
    unnamed x8, local copies, waits for them, and re-layouts  3.59 us
  transfers between devices with their start and end apart: 6, of which 3 were waited for; matrix products, arithmetic and copies ran while one was open for 0% of the time, Pallas kernels for 11%

profile of v2, /device:TPU:0, one launch (start us, length us, event | category | flops | bytes accessed | tf_op | source)
XLA Modules:
  0.0 51.8 jit_solution(300356688715385713)
XLA Ops:
  0.0 0.0 copy-start.3
  0.0 0.7 %copy-done.3 = s32[1,1,3]{2,1,0:T(1,128)S(1)} copy-done((s32[1,1,3]{2,1,0:T(1,128)S(1)}, s32[1,1,3]{2,1,0:T(1,128)}, u32[]{:S(2)}) %copy-start.3) | copy-done | bytes 36
  0.7 4.1 %collective-permute-start = (s32[3]{0:T(128)S(1)}, s32[3]{0:T(128)S(1)}, u32[]{:S(2)}, u32[]{:S(2)}) collective-permute-start(s32[3]{0:T(128)S(1)} %bitcast.2), channel_id=1, source_target_pairs={{8,0},{10,2},{12,4},{14,6},{0,8},{2,10},{4,12},{6,14},{9,1},{11,3}... | collective-permute-start | bytes 44 | tf_op jit(solution)/shard_map/ppermute | solution.py:488
  4.7 0.0 copy-start
  4.7 1.0 %copy-done = f32[2,256,256]{2,1,0:T(8,128)S(1)} copy-done((f32[2,256,256]{2,1,0:T(8,128)S(1)}, f32[2,256,256]{2,1,0:T(8,128)}, u32[]{:S(2)}) %copy-start) | copy-done | bytes 524312
  5.8 0.0 copy-start.1
  5.8 0.9 %copy-done.1 = f32[256,256]{1,0:T(8,128)S(1)} copy-done((f32[256,256]{1,0:T(8,128)S(1)}, f32[256,256]{1,0:T(8,128)}, u32[]{:S(2)}) %copy-start.1) | copy-done | bytes 262168
  6.7 0.0 copy-start.2
  6.7 0.9 %copy-done.2 = f32[256,256]{1,0:T(8,128)S(1)} copy-done((f32[256,256]{1,0:T(8,128)S(1)}, f32[256,256]{1,0:T(8,128)}, u32[]{:S(2)}) %copy-start.2) | copy-done | bytes 262168
  7.7 0.2 shard_map.46.state
  7.8 0.0 collective-permute-done.partner
  7.9 0.9 %shard_map.47 = (f32[5,32,256]{2,1,0:T(8,128)S(1)}, f32[5,16,256]{2,1,0:T(8,128)S(1)}) custom-call(s32[3]{0:T(128)S(1)} %bitcast.3, s32[3]{0:T(128)S(1)} %collective-permute-done.partner, f32[4,2,256,128]{3,2,1,0:T(8,128)S(1)} %shard_map.46.state), custom_call_target="tpu_custom_call" | custom-call | tf_op jit(solution)/shard_map/pallas_call | solution.py:515
  8.7 0.1 collective-permute-start.1
  8.8 1.4 %collective-permute-done.1.other = f32[5,32,256]{2,1,0:T(8,128)S(1)} collective-permute-done((f32[5,32,256]{2,1,0:T(8,128)S(1)}, f32[5,32,256]{2,1,0:T(8,128)S(1)}, u32[]{:S(2)}, u32[]{:S(2)}) %collective-permute-start.1) | collective-permute-done | bytes 163872 | tf_op jit(solution)/shard_map/ppermute | solution.py:492
  10.2 0.7 %collective-permute-start.2 = (f32[24,512]{1,0:T(8,128)S(1)}, f32[24,512]{1,0:T(8,128)S(1)}, u32[]{:S(2)}, u32[]{:S(2)}) collective-permute-start(f32[24,512]{1,0:T(8,128)S(1)} %shard_map.48), channel_id=1, source_target_pairs={{2,1},{4,3},{6,5},{8,7},{10,9},{12,11},{14,13},{1,2},{3,4},{5,6},{... | collective-permute-start | bytes 147464 | tf_op jit(solution)/shard_map/ppermute | solution.py:522
  10.9 0.0 collective-permute-done.2.came
  10.9 4.9 %collective-permute-start.3 = (f32[24,512]{1,0:T(8,128)S(1)}, f32[24,512]{1,0:T(8,128)S(1)}, u32[]{:S(2)}, u32[]{:S(2)}) collective-permute-start(f32[24,512]{1,0:T(8,128)S(1)} %collective-permute-done.2.came), channel_id=1, source_target_pairs={{0,1},{1,0},{2,3},{3,2},{4,5},{5,4},{6,7},{7,6},{8,9},{9,8},{10,11... | collective-permute-start | bytes 147464 | tf_op jit(solution)/shard_map/ppermute | solution.py:492
  15.8 0.9 %collective-permute-done.3.near = f32[24,512]{1,0:T(8,128)S(1)} collective-permute-done((f32[24,512]{1,0:T(8,128)S(1)}, f32[24,512]{1,0:T(8,128)S(1)}, u32[]{:S(2)}, u32[]{:S(2)}) %collective-permute-start.3) | collective-permute-done | bytes 49184 | tf_op jit(solution)/shard_map/ppermute | solution.py:492
  16.6 4.0 %shard_map.49 = (f32[5,2,160,128]{3,2,1,0:T(8,128)S(1)}, f32[2,3,64,128]{3,2,1,0:T(8,128)S(1)}) custom-call(s32[3]{0:T(128)S(1)} %bitcast.4, s32[3]{0:T(128)S(1)} %collective-permute-done.partner, f32[4,2,256,128]{3,2,1,0:T(8,128)S(1)} %shard_map.46.state, f32[5,32,256]{2,1,0:T(8,128)S(1)} %get-tuple-element.9.mine, ...), custom_call_target="tpu_custom_call" | custom-call | tf_op jit(solution)/shard_map/pallas_call | solution.py:525
  20.7 3.7 %shard_map.50.fixes = f32[4,3,8,128]{3,2,1,0:T(8,128)S(1)} custom-call(f32[5,32,256]{2,1,0:T(8,128)S(1)} %get-tuple-element.9.mine, f32[5,32,256]{2,1,0:T(8,128)S(1)} %collective-permute-done.1.other, f32[5,16,256]{2,1,0:T(8,128)S(1)} %get-tuple-element.10.inner, f32[24,512]{1,0:T(8,128)S(1)} %collective-permute-done.2.came, ...), custom_call_target="tpu_custom_call" | custom-call | tf_op jit(solution)/shard_map/pallas_call | solution.py:532
  24.4 3.9 %shard_map.51.after = f32[2,3,72,128]{3,2,1,0:T(8,128)S(1)} custom-call(s32[3]{0:T(128)S(1)} %bitcast.5, s32[3]{0:T(128)S(1)} %collective-permute-done.partner, f32[5,2,160,128]{3,2,1,0:T(8,128)S(1)} %get-tuple-element.12.start, f32[4,3,8,128]{3,2,1,0:T(8,128)S(1)} %shard_map.50.fixes), custom_call_target="tpu_custom_call" | custom-call | tf_op jit(solution)/shard_map/pallas_call | solution.py:541
  28.4 2.5 %collective-permute-start.5 = (f32[2,3,72,128]{3,2,1,0:T(8,128)S(1)}, f32[2,3,72,128]{3,2,1,0:T(8,128)S(1)}, u32[]{:S(2)}, u32[]{:S(2)}) collective-permute-start(f32[2,3,72,128]{3,2,1,0:T(8,128)S(1)} %shard_map.51.after), channel_id=1, source_target_pairs={{8,0},{10,2},{12,4},{14,6},{0,8},{2,10},{4,12},{6,14},{9,1},{11,3}... | collective-permute-start | bytes 663560 | tf_op jit(solution)/shard_map/ppermute | solution.py:488
  30.9 0.5 collective-permute-start.4
  31.3 5.5 %shard_map.52.kept = f32[2,3,128,128]{3,2,1,0:T(8,128)S(1)} custom-call(s32[3]{0:T(128)S(1)} %bitcast.6, s32[3]{0:T(128)S(1)} %collective-permute-done.partner, f32[4,2,256,128]{3,2,1,0:T(8,128)S(1)} %shard_map.46.state, f32[5,32,256]{2,1,0:T(8,128)S(1)} %get-tuple-element.9.mine, f32[24,512]{1,0:T(8,128)S(1)} %collective-permute-done.2.came, ...), custom_call_target="tpu_custom_call" | custom-call | tf_op jit(solution)/shard_map/pallas_call | solution.py:545
  36.9 13.3 %collective-permute-done.4.upper = f32[2,3,64,128]{3,2,1,0:T(8,128)S(1)} collective-permute-done((f32[2,3,64,128]{3,2,1,0:T(8,128)S(1)}, f32[2,3,64,128]{3,2,1,0:T(8,128)S(1)}, u32[]{:S(2)}, u32[]{:S(2)}) %collective-permute-start.4) | collective-permute-done | bytes 196640 | tf_op jit(solution)/shard_map/ppermute | solution.py:488
  50.2 0.0 collective-permute-done.5.lower
  50.2 1.6 %shard_map.53 = f32[3,3,128,128]{3,2,1,0:T(8,128)} custom-call(s32[3]{0:T(128)S(1)} %bitcast.7, s32[3]{0:T(128)S(1)} %collective-permute-done.partner, f32[2,3,128,128]{3,2,1,0:T(8,128)S(1)} %shard_map.52.kept, f32[2,3,64,128]{3,2,1,0:T(8,128)S(1)} %collective-permute-done.4.upper, f32[2,3,72,128]{3,2,1,0:T(8,128)S(1)} %collective-permute-done.5.lower), custom_call_target="tpu_custom_call" | custom-call | tf_op jit(solution)/shard_map/pallas_call | solution.py:551
  (1 shorter events, 0.0 us)
Async XLA Ops:
  0.0 0.7 %copy-start.3 = (s32[1,1,3]{2,1,0:T(1,128)S(1)}, s32[1,1,3]{2,1,0:T(1,128)}, u32[]{:S(2)}) copy-start(s32[1,1,3]{2,1,0:T(1,128)} %param.7) | copy-start | bytes 40
  0.7 7.2 %collective-permute-start = (s32[3]{0:T(128)S(1)}, s32[3]{0:T(128)S(1)}, u32[]{:S(2)}, u32[]{:S(2)}) collective-permute-start(s32[3]{0:T(128)S(1)} %bitcast.2), channel_id=1, source_target_pairs={{8,0},{10,2},{12,4},{14,6},{0,8},{2,10},{4,12},{6,14},{9,1},{11,3}... | collective-permute-start | bytes 44 | tf_op jit(solution)/shard_map/ppermute | solution.py:488
  4.7 1.0 %copy-start = (f32[2,256,256]{2,1,0:T(8,128)S(1)}, f32[2,256,256]{2,1,0:T(8,128)}, u32[]{:S(2)}) copy-start(f32[2,256,256]{2,1,0:T(8,128)} %velocity.1) | copy-start | bytes 1572868
  5.8 0.9 %copy-start.1 = (f32[256,256]{1,0:T(8,128)S(1)}, f32[256,256]{1,0:T(8,128)}, u32[]{:S(2)}) copy-start(f32[256,256]{1,0:T(8,128)} %depth.1) | copy-start | bytes 786436
  6.7 0.9 %copy-start.2 = (f32[256,256]{1,0:T(8,128)S(1)}, f32[256,256]{1,0:T(8,128)}, u32[]{:S(2)}) copy-start(f32[256,256]{1,0:T(8,128)} %bed.1) | copy-start | bytes 786436
  8.7 1.5 %collective-permute-start.1 = (f32[5,32,256]{2,1,0:T(8,128)S(1)}, f32[5,32,256]{2,1,0:T(8,128)S(1)}, u32[]{:S(2)}, u32[]{:S(2)}) collective-permute-start(f32[5,32,256]{2,1,0:T(8,128)S(1)} %get-tuple-element.9.mine), channel_id=1, source_target_pairs={{0,1},{1,0},{2,3},{3,2},{4,5},{5,4},{6,7},{7,6},{8,9},{9,8},{10,11... | collective-permute-start | bytes 491528 | tf_op jit(solution)/shard_map/ppermute | solution.py:492
  10.2 0.7 %collective-permute-start.2 = (f32[24,512]{1,0:T(8,128)S(1)}, f32[24,512]{1,0:T(8,128)S(1)}, u32[]{:S(2)}, u32[]{:S(2)}) collective-permute-start(f32[24,512]{1,0:T(8,128)S(1)} %shard_map.48), channel_id=1, source_target_pairs={{2,1},{4,3},{6,5},{8,7},{10,9},{12,11},{14,13},{1,2},{3,4},{5,6},{... | collective-permute-start | bytes 147464 | tf_op jit(solution)/shard_map/ppermute | solution.py:522
  10.9 5.8 %collective-permute-start.3 = (f32[24,512]{1,0:T(8,128)S(1)}, f32[24,512]{1,0:T(8,128)S(1)}, u32[]{:S(2)}, u32[]{:S(2)}) collective-permute-start(f32[24,512]{1,0:T(8,128)S(1)} %collective-permute-done.2.came), channel_id=1, source_target_pairs={{0,1},{1,0},{2,3},{3,2},{4,5},{5,4},{6,7},{7,6},{8,9},{9,8},{10,11... | collective-permute-start | bytes 147464 | tf_op jit(solution)/shard_map/ppermute | solution.py:492
  28.4 21.8 %collective-permute-start.5 = (f32[2,3,72,128]{3,2,1,0:T(8,128)S(1)}, f32[2,3,72,128]{3,2,1,0:T(8,128)S(1)}, u32[]{:S(2)}, u32[]{:S(2)}) collective-permute-start(f32[2,3,72,128]{3,2,1,0:T(8,128)S(1)} %shard_map.51.after), channel_id=1, source_target_pairs={{8,0},{10,2},{12,4},{14,6},{0,8},{2,10},{4,12},{6,14},{9,1},{11,3}... | collective-permute-start | bytes 663560 | tf_op jit(solution)/shard_map/ppermute | solution.py:488
  30.9 19.3 %collective-permute-start.4 = (f32[2,3,64,128]{3,2,1,0:T(8,128)S(1)}, f32[2,3,64,128]{3,2,1,0:T(8,128)S(1)}, u32[]{:S(2)}, u32[]{:S(2)}) collective-permute-start(f32[2,3,64,128]{3,2,1,0:T(8,128)S(1)} %get-tuple-element.11.after), channel_id=1, source_target_pairs={{8,0},{10,2},{12,4},{14,6},{0,8},{2,10},{4,12},{6,14},{9,1},{11,3}... | collective-permute-start | bytes 589832 | tf_op jit(solution)/shard_map/ppermute | solution.py:488

commit v3 on v2

v3 whole, which is shorter than its diff:
```python
import jax
import jax.numpy as jnp
from jax import lax
from jax.experimental import pallas as pl
from jax.experimental.pallas import tpu as pltpu
from jax.sharding import PartitionSpec as P


TILE = 128
RT = 2
CT = 2
SLOTS = 3
MOVED = RT * CT // 2
ROWS = RT * TILE
COLS = CT * TILE
PAD = 16
SEAM = 40
SEAM_DEEP = SEAM + 2 * PAD
SPAN = TILE + 2 * PAD
INNER = 80
OUTER = TILE - INNER
REACH = 4
UNROLL_INNER = 3
UNROLL_OUTER = 2
UNROLL_FULL = 3
UNROLL_SEAM = 1

GRAVITY = 9.81
TIME_STEP = 0.04
DRY_DEPTH = 0.05
SPEED_FLOOR = 0.5
ROOT_GRAVITY = GRAVITY**0.5
TINY = 1.2e-38

VMEM = pl.BlockSpec(memory_space=pltpu.VMEM)
HBM = pl.BlockSpec(memory_space=pltpu.HBM)
SMEM = pl.BlockSpec(memory_space=pltpu.SMEM)


def f32(*shape):
    return jax.ShapeDtypeStruct(shape, jnp.float32)


def call(kernel, ins, outs, scratch=(), room=20 * 2**20):
    return pl.pallas_call(
        kernel,
        in_specs=list(ins),
        out_specs=tuple(VMEM for _ in outs),
        out_shape=tuple(outs),
        scratch_shapes=list(scratch),
        compiler_params=pltpu.CompilerParams(vmem_limit_bytes=room),
    )


def limited(down, up):
    return 0.5 * jnp.maximum(jnp.minimum(down, jnp.maximum(up, 0.0)), jnp.minimum(up, 0.0))


def speeds(water, normal, across):
    square = water * water
    factor = (water + water) / (square + jnp.maximum(square, DRY_DEPTH * DRY_DEPTH))
    return factor * normal, factor * across


def wave_speed(level):
    return (ROOT_GRAVITY * level) * lax.rsqrt(jnp.maximum(level, TINY))


def face_flux(left, right):
    water_l, speed_l, drift_l, ground_l = left
    water_r, speed_r, drift_r, ground_r = right
    top = jnp.maximum(ground_l, ground_r)
    level_l = jnp.maximum(water_l + (ground_l - top), 0.0)
    level_r = jnp.maximum(water_r + (ground_r - top), 0.0)
    wave_l = wave_speed(level_l)
    wave_r = wave_speed(level_r)
    lower = jnp.minimum(jnp.minimum(speed_l - wave_l, speed_r - wave_r), 0.0)
    upper = jnp.maximum(jnp.maximum(speed_l + wave_l, speed_r + wave_r), 0.0)
    inverse = 1.0 / jnp.maximum(upper - lower, SPEED_FLOOR)
    up = upper * inverse
    low = lower * inverse
    both = upper * low
    part_l = level_l * (up * speed_l - both)
    part_r = level_r * (both - low * speed_r)
    press_l = (0.5 * GRAVITY) * (level_l * level_l)
    press_r = (0.5 * GRAVITY) * (level_r * level_r)
    mass = part_l + part_r
    push = part_l * speed_l + part_r * speed_r + up * press_l - low * press_r
    side = part_l * drift_l + part_r * drift_r
    return mass, push - press_l, push - press_r, side


def sweep(src, ground, dst, width, steps, starts, lane_flow, row_flow, unroll, flush):
    sub = lax.broadcasted_iota(jnp.int32, (8, 128), 0)
    cols = range(width)

    def step(i, carry):
        shift = pl.multiple_of(i * 8, 8)

        def read(f, w, offset):
            held = src if f < 3 else ground
            return held[f, w, pl.ds(shift + starts[w] + offset, 8), :]

        now = []
        for w in cols:
            x = [read(f, w, 0) for f in range(4)]
            low, high, half = [], [], []
            for f in (0, lane_flow, row_flow, 3):
                down = x[f] - pltpu.roll(x[f], 1, 1)
                hs = limited(down, pltpu.roll(down, TILE - 1, 1))
                low.append(x[f] - hs)
                high.append(x[f] + hs)
                half.append(hs)
            fast = speeds(high[0], high[1], high[2])
            slow = speeds(low[0], low[1], low[2])
            left = [pltpu.roll(v, 1, 1) for v in (high[0], fast[0], fast[1], high[3])]
            mass, push_l, push_r, side = face_flux(left, (low[0], slow[0], slow[1], low[3]))
            weight = (2.0 * GRAVITY) * x[0]
            gain_water = mass - pltpu.roll(mass, TILE - 1, 1)
            gain_lane = push_r - pltpu.roll(push_l, TILE - 1, 1) - weight * (half[0] + half[3])
            gain_row = side - pltpu.roll(side, TILE - 1, 1)
            low, high, half = [], [], []
            for f in (0, row_flow, lane_flow, 3):
                hs = limited(x[f] - read(f, w, -1), read(f, w, 1) - x[f])
                low.append(x[f] - hs)
                high.append(x[f] + hs)
                half.append(hs)
            fast = speeds(high[0], high[1], high[2])
            slow = speeds(low[0], low[1], low[2])
            old_high, old_flux, old_gain = carry[w]
            high_now = tuple(pltpu.roll(v, 1, 0) for v in (high[0], fast[0], fast[1], high[3]))
            left = [jnp.where(sub == 0, o, n) for o, n in zip(old_high, high_now)]
            mass, push_l, push_r, side = face_flux(left, (low[0], slow[0], slow[1], low[3]))
            gain = (
                gain_water + mass,
                gain_lane + side,
                gain_row + push_r - weight * (half[0] + half[3]),
            )
            flux_now = tuple(pltpu.roll(v, 7, 0) for v in (mass, side, push_l))
            for f, g, o, n in zip((0, lane_flow, row_flow), old_gain, old_flux, flux_now):
                dst[f, w, pl.ds(shift + starts[w] - 8, 8), :] = read(f, w, -8) + TIME_STEP * (
                    g - jnp.where(sub == 7, n, o)
                )
            now.append((high_now, flux_now, gain))
        return tuple(now)

    zero = jnp.zeros((8, 128), jnp.float32)
    start = tuple(((zero,) * 4, (zero,) * 3, (zero,) * 3) for _ in cols)
    carry = lax.fori_loop(0, steps, step, start, unroll=unroll)
    if flush:
        for w in cols:
            rows = pl.ds(starts[w] + 8 * (steps - 1), 8)
            _, old_flux, old_gain = carry[w]
            for f, g, o in zip((0, lane_flow, row_flow), old_gain, old_flux):
                dst[f, w, rows, :] = src[f, w, rows, :] + TIME_STEP * (g - o)


def load_kernel(depth, velocity, bed, state, turned, water, speed, ground, sems):
    copies = [
        pltpu.make_async_copy(depth, water, sems.at[0]),
        pltpu.make_async_copy(velocity, speed, sems.at[1]),
        pltpu.make_async_copy(bed, ground, sems.at[2]),
    ]
    for copy in copies:
        copy.start()
    for copy in copies:
        copy.wait()
    for w in range(CT):
        cols = slice(w * TILE, (w + 1) * TILE)
        for r in range(0, ROWS, 8):
            rows = slice(r, r + 8)
            here = water[rows, cols]
            state[0, w, rows, :] = here
            state[1, w, rows, :] = here * speed[0, rows, cols]
            state[2, w, rows, :] = here * speed[1, rows, cols]
            state[3, w, rows, :] = ground[rows, cols]
    lane = lax.broadcasted_iota(jnp.int32, (TILE, TILE), 1)
    for f in range(4):
        for r in range(RT):
            held = slice(r * TILE, (r + 1) * TILE)
            one, two = state[f, 0, held, :], state[f, CT - 1, held, :]
            flipped = jnp.where(lane < TILE // 2, one, two).T
            turned[f, 0:8, held] = flipped[TILE - 8 :, :]
            turned[f, 8:16, held] = flipped[:8, :]
            flipped = jnp.where(lane < TILE // 2, two, one).T
            turned[f, 16:24, held] = flipped[TILE - 8 :, :]
            turned[f, 24:32, held] = flipped[:8, :]


class Lists:
    def __init__(self, lists):
        self.rows = lax.axis_index("rows")
        self.cols = lax.axis_index("cols")
        self.span = CT * lax.axis_size("cols")
        self.ids = [
            (self.rows * RT + t // CT) * self.span + self.cols * CT + t % CT for t in range(RT * CT)
        ]
        self.listed = [lists[k] for k in range(SLOTS)]
        self.partner = [lists[SLOTS + k] for k in range(SLOTS)]

    def inside(self, entry):
        found = [entry == i for i in self.ids]
        any_found = found[0]
        local = jnp.int32(0)
        for t in range(1, RT * CT):
            any_found = any_found | found[t]
            local = jnp.where(found[t], jnp.int32(t), local)
        return any_found, local

    def active(self, t):
        hit = self.listed[0] == self.ids[t]
        for entry in self.listed[1:] + self.partner:
            hit = hit | (entry == self.ids[t])
        return hit

    def flags(self):
        return [jnp.where(self.active(t), 1.0, 0.0) for t in range(RT * CT)]

    def outgoing(self):
        used = [jnp.bool_(False)] * MOVED
        tile = [jnp.int32(0)] * MOVED
        rank = jnp.int32(0)
        for entry in self.partner:
            own, local = self.inside(entry)
            for k in range(MOVED):
                take = own & (rank == k)
                used[k] = used[k] | take
                tile[k] = jnp.where(take, local, tile[k])
            rank = rank + own.astype(jnp.int32)
        return used, tile

    def kept(self):
        used = [jnp.bool_(False)] * MOVED
        tile = [jnp.int32(0)] * MOVED
        rank = jnp.int32(0)
        for entry in self.listed:
            own, local = self.inside(entry)
            for k in range(MOVED):
                take = own & (rank == k)
                used[k] = used[k] | take
                tile[k] = jnp.where(take, local, tile[k])
            rank = rank + own.astype(jnp.int32)
        return used, tile


def edge_kernel(lists, state, turned, own, out):
    lists = Lists(lists)
    is_left = lists.cols == 0
    flags = lists.flags()
    for w in range(CT):
        cols = slice(w * TILE, (w + 1) * TILE)
        for f in range(4):
            rows = slice(4 * f, 4 * f + 4)
            first = state[f, w, 0:REACH, :]
            last = state[f, w, ROWS - REACH : ROWS, :]
            own[rows, cols] = jnp.where(is_left, first, last)
            out[rows, cols] = jnp.where(is_left, last, first)
        first, last = flags[w], flags[(RT - 1) * CT + w]
        own[16:24, cols] = jnp.full((8, TILE), jnp.where(is_left, first, last), jnp.float32)
        out[16:24, cols] = jnp.full((8, TILE), jnp.where(is_left, last, first), jnp.float32)
    for f in range(4):
        rows = slice(24 + 4 * f, 28 + 4 * f)
        out[rows, :] = jnp.where(is_left, turned[f, 4:8, :], turned[f, 8:12, :])
    for r in range(RT):
        flag = jnp.where(is_left, flags[r * CT + CT - 1], flags[r * CT])
        out[40:48, r * TILE : (r + 1) * TILE] = jnp.full((8, TILE), flag, jnp.float32)


def wide_kernel(own, other, out):
    is_left = lax.axis_index("cols") == 0
    near = other[0:24, :]
    out[:, 0:COLS] = jnp.where(is_left, own[...], near)
    out[:, COLS : 2 * COLS] = jnp.where(is_left, near, own[...])


def halo_pieces(came, near, f, upper):
    is_left = lax.axis_index("cols") == 0
    rows = slice(4 * f, 4 * f + 4)
    halo = jnp.where(is_left == upper, came[rows, :], near[rows, :])
    part = [halo[:, q * TILE : (q + 1) * TILE] for q in range(2 * CT)]
    return (
        jnp.where(is_left, part[0], part[2]),
        jnp.where(is_left, part[1], part[3]),
        jnp.where(is_left, part[2], part[1]),
    )


def gather_pair(tile, flags, state, start, halos):
    blank = jnp.zeros((4, TILE), jnp.float32)
    over = slice(PAD - 8, PAD)
    under = slice(PAD + TILE, PAD + TILE + 8)
    for k in range(MOVED):
        r, c = tile[k] // CT, tile[k] % CT
        base = pl.multiple_of(r * TILE, TILE)
        for f in range(4):
            start[f, k, PAD : PAD + TILE, :] = state[f, c, pl.ds(base, TILE), :]
        if halos is not None:
            ends = [
                [jnp.where(c == 0, *halo_pieces(*halos, f, upper)[:2]) for f in range(5)]
                for upper in (True, False)
            ]

        @pl.when(r == 0)
        def _(k=k, c=c):
            for f in range(4):
                start[f, k, under, :] = state[f, c, TILE : TILE + 8, :]
            flag = jnp.where(c == 0, flags[CT], flags[CT + 1])
            start[4, k, under, :] = jnp.full((8, TILE), flag, jnp.float32)
            if halos is not None:
                for f in range(5):
                    start[f, k, PAD - 8 : PAD - 4, :] = blank
                    start[f, k, PAD - 4 : PAD, :] = ends[0][f]

        @pl.when(r == RT - 1)
        def _(k=k, c=c):
            for f in range(4):
                start[f, k, over, :] = state[f, c, TILE - 8 : TILE, :]
            flag = jnp.where(c == 0, flags[0], flags[1])
            start[4, k, over, :] = jnp.full((8, TILE), flag, jnp.float32)
            if halos is not None:
                for f in range(5):
                    start[f, k, PAD + TILE : PAD + TILE + 4, :] = ends[1][f]
                    start[f, k, PAD + TILE + 4 : PAD + TILE + 8, :] = blank


def still(dst, src, width, rows):
    for w in range(width):
        alive = src[4, w, rows, :] > 0.5
        for f in range(3):
            dst[f, w, rows, :] = jnp.where(alive, dst[f, w, rows, :], src[f, w, rows, :])


def aligned(row):
    return row if isinstance(row, int) else pl.multiple_of(row, 8)


def advance_pair(start, middle, end, firsts, count, masked, unroll):
    steps = count // 8 + 2
    starts = [aligned(first) + (PAD - 8) for first in firsts]
    sweep(start, start, middle, MOVED, steps, starts, 1, 2, unroll, True)
    for w in range(MOVED):
        for row in masked[w]:
            rows = pl.ds(aligned(row) + PAD, 8)
            alive = start[4, w, rows, :] > 0.5
            for f in range(3):
                middle[f, w, rows, :] = jnp.where(alive, middle[f, w, rows, :], start[f, w, rows, :])
    sweep(middle, start, end, MOVED, steps, starts, 1, 2, unroll, False)


def overlay(cell, fix, board, store):
    lane = lax.broadcasted_iota(jnp.int32, (8, TILE), 1)
    for f in range(3):
        board[8 * f : 8 * f + 8, :] = fix(f)
    turned = board[...].T
    for f in range(3):
        for b in range(0, TILE, 8):
            strip = turned[b : b + 8, :]
            left = pltpu.roll(strip, (TILE - 8 * f) % TILE, 1)
            right = pltpu.roll(strip, TILE - 8 - 8 * f, 1)
            value = jnp.where(lane < REACH, left, cell(f, b))
            store(f, b, jnp.where(lane >= TILE - REACH, right, value))


def inner_kernel(lists, state, out, start, middle, end):
    lists = Lists(lists)
    _, tile = lists.outgoing()
    gather_pair(tile, lists.flags(), state, start, None)
    top = [t // CT == 0 for t in tile]
    firsts = [jnp.where(u, OUTER, 0) for u in top]
    masked = [[jnp.where(u, TILE, -8)] for u in top]
    advance_pair(start, middle, end, firsts, INNER, masked, UNROLL_INNER)
    for k in range(MOVED):
        rows = pl.ds(pl.multiple_of(firsts[k], 8) + PAD, INNER)
        for f in range(3):
            out[k, f] = end[f, k, rows, :]


def outer_kernel(lists, state, came, near, fixes, out, start, middle, end):
    lists = Lists(lists)
    _, tile = lists.outgoing()
    gather_pair(tile, lists.flags(), state, start, (came, near))
    top = [t // CT == 0 for t in tile]
    firsts = [jnp.where(u, 0, INNER) for u in top]
    masked = [[jnp.where(u, -8, TILE)] for u in top]
    advance_pair(start, middle, end, firsts, OUTER, masked, UNROLL_OUTER)
    for k in range(MOVED):
        rows = pl.ds(pl.multiple_of(firsts[k], 8) + PAD, OUTER)
        for f in range(3):
            out[k, f, 0:OUTER, :] = end[f, k, rows, :]
            out[k, f, OUTER : OUTER + 8, :] = fixes[tile[k], f]


def keep_kernel(lists, state, came, near, fixes, out, start, middle, end, board):
    lists = Lists(lists)
    used, tile = lists.kept()

    @pl.when(used[0])
    def _():
        gather_pair(tile, lists.flags(), state, start, (came, near))
        masked = [[-8, TILE]] * MOVED
        advance_pair(start, middle, end, [0] * MOVED, TILE, masked, UNROLL_FULL)
        board[...] = jnp.zeros_like(board)
        for k in range(MOVED):

            def store(f, b, value, k=k):
                out[k, f, b : b + 8, :] = value

            overlay(
                lambda f, b, k=k: end[f, k, PAD + b : PAD + b + 8, :],
                lambda f, k=k: fixes[tile[k], f],
                board,
                store,
            )


def seam_kernel(lists, turned, other, came, near, fixes, start, middle, end, one, two, side, board):
    lists = Lists(lists)
    is_left = lists.cols == 0
    flags = lists.flags()
    lane = lax.broadcasted_iota(jnp.int32, (8, TILE), 1)
    for w in range(CT):
        cols = slice(w * TILE, (w + 1) * TILE)
        for f in range(5):
            beside = other[24 + 4 * f : 28 + 4 * f, cols]
            start[f, w, PAD + 8 : PAD + 12, :] = jnp.where(is_left, beside, 0.0)
            start[f, w, PAD + 12 : PAD + 16, :] = jnp.where(is_left, 0.0, beside)
            if f < 4:
                start[f, w, PAD : PAD + 8, :] = turned[f, 0:8, cols]
                start[f, w, PAD + 16 : PAD + 40, :] = turned[f, 8:32, cols]
        for row, c in ((0, CT - 1), (16, 0), (24, 0), (32, CT - 1)):
            full = jnp.full((8, TILE), flags[w * CT + c], jnp.float32)
            start[4, w, PAD + row : PAD + row + 8, :] = full
    for f in range(5):
        for place, upper in ((0, False), (4, True)):
            rows = slice(8 * f + place, 8 * f + place + 4)
            pieces = halo_pieces(came, near, f, upper)
            one[rows, :], two[rows, :], side[rows, :] = pieces
    board[...] = jnp.zeros_like(board)
    for b in range(0, 40, 8):
        rows = slice(b, b + 8)
        first, second, beside = one[rows, :], two[rows, :], side[rows, :]
        value = jnp.where(lane < 8, pltpu.roll(second, 8, 1), 0.0)
        value = jnp.where((lane >= 8) & (lane < 12) & is_left, pltpu.roll(beside, 8, 1), value)
        far = jnp.logical_not(is_left)
        value = jnp.where((lane >= 12) & (lane < 16) & far, pltpu.roll(beside, 16, 1), value)
        value = jnp.where((lane >= 16) & (lane < 24), pltpu.roll(first, 16, 1), value)
        value = jnp.where((lane >= 24) & (lane < 32), pltpu.roll(first, 32, 1), value)
        board[rows, :] = jnp.where((lane >= 32) & (lane < 40), pltpu.roll(second, 32, 1), value)
    turned = board[...].T
    for f in range(5):
        for b in range(0, SEAM, 8):
            rows = slice(PAD + b, PAD + b + 8)
            first, second = start[f, 0, rows, :], start[f, 1, rows, :]
            ends = pltpu.roll(turned[b : b + 8, :], (8 - 8 * f) % TILE, 1)
            value = jnp.where(lane < 8, pltpu.roll(second, 8, 1), 0.0)
            value = jnp.where((lane >= 8) & (lane < 16), ends, value)
            value = jnp.where((lane >= 16) & (lane < 24), pltpu.roll(first, 16, 1), value)
            value = jnp.where((lane >= 24) & (lane < 32), pltpu.roll(first, 32, 1), value)
            start[f, CT, rows, :] = jnp.where(
                (lane >= 32) & (lane < 40), pltpu.roll(second, 32, 1), value
            )
    width = CT + 1
    sweep(start, start, middle, width, SEAM // 8, [PAD] * width, 2, 1, UNROLL_SEAM, True)
    still(middle, start, width, slice(PAD, PAD + SEAM))
    sweep(middle, start, end, width, SEAM // 8, [PAD] * width, 2, 1, UNROLL_SEAM, True)
    lane = lax.broadcasted_iota(jnp.int32, (4, TILE), 1)
    for t in range(RT * CT):
        r, c = t // CT, t % CT
        for place, row in ((0, 16 if c == 0 else 32), (4, 28 if c == 0 else 4)):
            rows = slice(PAD + row, PAD + row + 4)
            for f in range(3):
                ends = end[f, CT, rows, :]
                low = pltpu.roll(ends, 112 if r == 0 else 96, 1)
                high = pltpu.roll(ends, 96 if r == 0 else 120, 1)
                value = jnp.where(lane < REACH, low, end[f, r, rows, :])
                fixes[t, f, place : place + 4, :] = jnp.where(lane >= TILE - REACH, high, value)


def pack_kernel(lists, kept, inner, outer, packed, board):
    lists = Lists(lists)
    board[...] = jnp.zeros_like(board)
    far = jnp.int32(0)
    near = jnp.int32(0)
    for s in range(SLOTS):
        entry = lists.listed[s]
        own, _ = lists.inside(entry)
        foreign = (entry >= 0) & jnp.logical_not(own)
        top = lax.rem(lax.div(jnp.maximum(entry, 0), lists.span), RT) == 0
        here = jnp.minimum(near, MOVED - 1)
        there = jnp.minimum(far, MOVED - 1)
        near = near + own.astype(jnp.int32)
        far = far + foreign.astype(jnp.int32)

        @pl.when(own)
        def _(s=s, here=here):
            packed[s] = kept[here]

        @pl.when(foreign)
        def _(s=s, there=there, top=top):
            def cell(f, b):
                high = jnp.where(top, b - OUTER, b)
                low = jnp.where(top, b, b - INNER)
                high = pl.multiple_of(jnp.clip(high, 0, INNER - 8), 8)
                low = pl.multiple_of(jnp.clip(low, 0, OUTER - 8), 8)
                within = jnp.where(top, b >= OUTER, b < INNER)
                return jnp.where(
                    within, inner[there, f, pl.ds(high, 8), :], outer[there, f, pl.ds(low, 8), :]
                )

            def store(f, b, value):
                packed[s, f, b : b + 8, :] = value

            overlay(cell, lambda f: outer[there, f, OUTER : OUTER + 8, :], board, store)

        @pl.when(entry < 0)
        def _(s=s):
            packed[s] = jnp.zeros((3, TILE, TILE), jnp.float32)


def passed_along(block, distance):
    count = lax.axis_size("rows")
    return lax.ppermute(block, "rows", [((i - distance) % count, i) for i in range(count)])


def swapped(block):
    return lax.ppermute(block, "cols", [(0, 1), (1, 0)])


def scratch(*shape):
    return pltpu.VMEM(shape, jnp.float32)


def shards(depth, velocity, bed, slots):
    count = lax.axis_size("rows")
    half = count // 2
    listed = slots[0, 0]
    partner = passed_along(listed, half)
    state, turned = call(
        load_kernel,
        [HBM] * 3,
        [f32(4, CT, ROWS, TILE), f32(4, 32, ROWS)],
        [
            scratch(ROWS, COLS),
            scratch(2, ROWS, COLS),
            scratch(ROWS, COLS),
            pltpu.SemaphoreType.DMA((3,)),
        ],
    )(depth, velocity, bed)
    lists = jnp.concatenate([listed, partner])
    own, beside = call(edge_kernel, [SMEM, VMEM, VMEM], [f32(24, COLS), f32(48, COLS)])(
        lists, state, turned
    )
    other = swapped(beside)
    (wide,) = call(wide_kernel, [VMEM, VMEM], [f32(24, 2 * COLS)])(own, other)
    route = [(2 * r, 2 * r - 1) for r in range(1, count)]
    route += [(2 * r + 1, 2 * r + 2) for r in range(count - 1)]
    came = lax.ppermute(wide, ("rows", "cols"), route)
    pair = [scratch(3, MOVED, SPAN, TILE)] * 2
    gathered = [scratch(5, MOVED, SPAN, TILE)]
    (inner,) = call(
        inner_kernel, [SMEM, VMEM], [f32(MOVED, 3, INNER, TILE)], gathered + pair
    )(lists, state)
    far_inner = passed_along(inner, half)
    near = swapped(came)
    (fixes,) = call(
        seam_kernel,
        [SMEM] + [VMEM] * 4,
        [f32(RT * CT, 3, 8, TILE)],
        [scratch(5, CT + 1, SEAM_DEEP, TILE)]
        + [scratch(3, CT + 1, SEAM_DEEP, TILE)] * 2
        + [scratch(40, TILE)] * 3
        + [scratch(TILE, TILE)],
    )(lists, turned, other, came, near)
    (outer,) = call(
        outer_kernel, [SMEM] + [VMEM] * 4, [f32(MOVED, 3, OUTER + 8, TILE)], gathered + pair
    )(lists, state, came, near, fixes)
    far_outer = passed_along(outer, half)
    (kept,) = call(
        keep_kernel,
        [SMEM] + [VMEM] * 4,
        [f32(MOVED, 3, TILE, TILE)],
        gathered + pair + [scratch(TILE, TILE)],
    )(lists, state, came, near, fixes)
    (packed,) = call(
        pack_kernel, [SMEM] + [VMEM] * 3, [f32(SLOTS, 3, TILE, TILE)], [scratch(TILE, TILE)]
    )(lists, kept, far_inner, far_outer)
    return packed[None, None]


def solution(mesh):
    in_specs = (
        P(("groups", "rows"), "cols"),
        P(None, ("groups", "rows"), "cols"),
        P(("groups", "rows"), "cols"),
        P(("groups", "rows"), "cols", None),
    )
    out_specs = P(("groups", "rows"), "cols", None, None, None, None)

    return jax.shard_map(shards, mesh=mesh, in_specs=in_specs, out_specs=out_specs, check_vma=False)
```

time: 52 us -> 40.9 us (0.79)
  waiting for transfers between devices: 15.6 us -> 7.33 us
  starting transfers between devices: 12.7 us -> 10.1 us
    ppermute x3, waiting for transfers between devices: 13.3 us -> 4.88 us  [passed_along(): lax.ppermute(block, 'rows', [((i - distance) % count, i) for i in range(c...]
    ppermute x2, starting transfers between devices: 4.94 us -> 0.07 us  [swapped(): return lax.ppermute(block, 'cols', [(0, 1), (1, 0)])]
    ppermute x3, starting transfers between devices: 7.05 us -> 9.35 us  [passed_along(): lax.ppermute(block, 'rows', [((i - distance) % count, i) for i in range(c...]
  transfers between devices with their start and end apart: 6 -> 6, of which waited for: 3 -> 3; matrix products, arithmetic and copies ran while one was open for 0% -> 0% of each run, Pallas kernels for 11% -> 42%
where the time goes in v3:
time: 40.9 us; the launch traced here: 40.6 us
  Pallas kernels  19.5 us (48%)
  starting transfers between devices  10.1 us (25%)
  waiting for transfers between devices  7.33 us (18%)
  local copies, waits for them, and re-layouts  3.59 us (9%)
    ppermute x3, starting transfers between devices, passed_along(): lax.ppermute(block, 'rows', [((i - distance) % count, i) for i in range(c...  9.35 us
    pallas_call x1, Pallas kernels, shards(): call(keep_kernel, [SMEM] + [VMEM] * 4, [f32(MOVED, 3, TILE, TILE)], gathe...  5.47 us
    ppermute x3, waiting for transfers between devices, passed_along(): lax.ppermute(block, 'rows', [((i - distance) % count, i) for i in range(c...  4.88 us
    pallas_call x1, Pallas kernels, shards(): call(seam_kernel, [SMEM] + [VMEM] * 4, [f32(RT * CT, 3, 8, TILE)], [scrat...  4.26 us
    pallas_call x1, Pallas kernels, shards(): call(inner_kernel, [SMEM, VMEM], [f32(MOVED, 3, INNER, TILE)], gathered +...  3.71 us
    unnamed x8, local copies, waits for them, and re-layouts  3.59 us
    pallas_call x1, Pallas kernels, shards(): call(outer_kernel, [SMEM] + [VMEM] * 4, [f32(MOVED, 3, OUTER + 8, TILE)],...  3.34 us
    ppermute x2, waiting for transfers between devices, swapped(): return lax.ppermute(block, 'cols', [(0, 1), (1, 0)])  2.45 us
  transfers between devices with their start and end apart: 6, of which 3 were waited for; matrix products, arithmetic and copies ran while one was open for 0% of the time, Pallas kernels for 42%

profile of v3, /device:TPU:0, one launch (start us, length us, event | category | flops | bytes accessed | tf_op | source)
XLA Modules:
  0.0 40.6 jit_solution(15253045833941686901)
XLA Ops:
  0.0 0.0 copy-start.3
  0.0 0.7 %copy-done.3 = s32[1,1,3]{2,1,0:T(1,128)S(1)} copy-done((s32[1,1,3]{2,1,0:T(1,128)S(1)}, s32[1,1,3]{2,1,0:T(1,128)}, u32[]{:S(2)}) %copy-start.3) | copy-done | bytes 36
  0.7 4.1 %collective-permute-start = (s32[3]{0:T(128)S(1)}, s32[3]{0:T(128)S(1)}, u32[]{:S(2)}, u32[]{:S(2)}) collective-permute-start(s32[3]{0:T(128)S(1)} %bitcast.2), channel_id=1, source_target_pairs={{8,0},{10,2},{12,4},{14,6},{0,8},{2,10},{4,12},{6,14},{9,1},{11,3}... | collective-permute-start | bytes 44 | tf_op jit(solution)/shard_map/ppermute | solution.py:522
  4.7 0.0 copy-start
  4.7 1.0 %copy-done = f32[2,256,256]{2,1,0:T(8,128)S(1)} copy-done((f32[2,256,256]{2,1,0:T(8,128)S(1)}, f32[2,256,256]{2,1,0:T(8,128)}, u32[]{:S(2)}) %copy-start) | copy-done | bytes 524312
  5.8 0.0 copy-start.1
  5.8 0.9 %copy-done.1 = f32[256,256]{1,0:T(8,128)S(1)} copy-done((f32[256,256]{1,0:T(8,128)S(1)}, f32[256,256]{1,0:T(8,128)}, u32[]{:S(2)}) %copy-start.1) | copy-done | bytes 262168
  6.7 0.0 copy-start.2
  6.7 0.9 %copy-done.2 = f32[256,256]{1,0:T(8,128)S(1)} copy-done((f32[256,256]{1,0:T(8,128)S(1)}, f32[256,256]{1,0:T(8,128)}, u32[]{:S(2)}) %copy-start.2) | copy-done | bytes 262168
  7.7 0.4 %shard_map.46 = (f32[4,2,256,128]{3,2,1,0:T(8,128)S(1)}, f32[4,32,256]{2,1,0:T(8,128)S(1)}) custom-call(f32[256,256]{1,0:T(8,128)S(1)} %copy-done.1, f32[2,256,256]{2,1,0:T(8,128)S(1)} %copy-done, f32[256,256]{1,0:T(8,128)S(1)} %copy-done.2), custom_call_target="tpu_custom_call" | custom-call | tf_op jit(solution)/shard_map/pallas_call | solution.py:538
  8.1 0.0 collective-permute-done
  8.1 0.1 pad_add_fusion.lists
  8.2 0.6 %shard_map.47 = (f32[24,256]{1,0:T(8,128)S(1)}, f32[48,256]{1,0:T(8,128)S(1)}) custom-call(s32[6]{0:T(128)S(1)} %pad_add_fusion.lists, f32[4,2,256,128]{3,2,1,0:T(8,128)S(1)} %get-tuple-element.9.state, f32[4,32,256]{2,1,0:T(8,128)S(1)} %get-tuple-element.10.turned), custom_call_target="tpu_custom_call" | custom-call | tf_op jit(solution)/shard_map/pallas_call | solution.py:550
  8.8 0.1 collective-permute-start.1
  8.9 1.2 %collective-permute-done.1.other = f32[48,256]{1,0:T(8,128)S(1)} collective-permute-done((f32[48,256]{1,0:T(8,128)S(1)}, f32[48,256]{1,0:T(8,128)S(1)}, u32[]{:S(2)}, u32[]{:S(2)}) %collective-permute-start.1) | collective-permute-done | bytes 49184 | tf_op jit(solution)/shard_map/ppermute | solution.py:526
  10.1 0.7 %collective-permute-start.2 = (f32[24,512]{1,0:T(8,128)S(1)}, f32[24,512]{1,0:T(8,128)S(1)}, u32[]{:S(2)}, u32[]{:S(2)}) collective-permute-start(f32[24,512]{1,0:T(8,128)S(1)} %shard_map.48), channel_id=1, source_target_pairs={{2,1},{4,3},{6,5},{8,7},{10,9},{12,11},{14,13},{1,2},{3,4},{5,6},{... | collective-permute-start | bytes 147464 | tf_op jit(solution)/shard_map/ppermute | solution.py:557
  10.8 3.7 %shard_map.51 = f32[2,3,80,128]{3,2,1,0:T(8,128)S(1)} custom-call(s32[6]{0:T(128)S(1)} %pad_add_fusion.lists, f32[4,2,256,128]{3,2,1,0:T(8,128)S(1)} %get-tuple-element.9.state), custom_call_target="tpu_custom_call" | custom-call | tf_op jit(solution)/shard_map/pallas_call | solution.py:560
  14.5 5.1 %collective-permute-start.4 = (f32[2,3,80,128]{3,2,1,0:T(8,128)S(1)}, f32[2,3,80,128]{3,2,1,0:T(8,128)S(1)}, u32[]{:S(2)}, u32[]{:S(2)}) collective-permute-start(f32[2,3,80,128]{3,2,1,0:T(8,128)S(1)} %shard_map.51), channel_id=1, source_target_pairs={{8,0},{10,2},{12,4},{14,6},{0,8},{2,10},{4,12},{6,14},{9,1},{11,3}... | collective-permute-start | bytes 737288 | tf_op jit(solution)/shard_map/ppermute | solution.py:522
  19.5 0.0 collective-permute-done.2.came
  19.5 0.0 collective-permute-start.3
  19.6 1.2 %collective-permute-done.3.near = f32[24,512]{1,0:T(8,128)S(1)} collective-permute-done((f32[24,512]{1,0:T(8,128)S(1)}, f32[24,512]{1,0:T(8,128)S(1)}, u32[]{:S(2)}, u32[]{:S(2)}) %collective-permute-start.3) | collective-permute-done | bytes 49184 | tf_op jit(solution)/shard_map/ppermute | solution.py:526
  20.8 4.3 %shard_map.49.fixes = f32[4,3,8,128]{3,2,1,0:T(8,128)S(1)} custom-call(s32[6]{0:T(128)S(1)} %pad_add_fusion.lists, f32[4,32,256]{2,1,0:T(8,128)S(1)} %get-tuple-element.10.turned, f32[48,256]{1,0:T(8,128)S(1)} %collective-permute-done.1.other, f32[24,512]{1,0:T(8,128)S(1)} %collective-permute-done.2.came, f32[24,512]{1,0:T(8,128)S(1)} %collective-permute-done.3.near), custom_call_target="tpu_custom_call" | custom-call | tf_op jit(solution)/shard_map/pallas_call | solution.py:565
  25.0 3.3 %shard_map.52 = f32[2,3,56,128]{3,2,1,0:T(8,128)S(1)} custom-call(s32[6]{0:T(128)S(1)} %pad_add_fusion.lists, f32[4,2,256,128]{3,2,1,0:T(8,128)S(1)} %get-tuple-element.9.state, f32[24,512]{1,0:T(8,128)S(1)} %collective-permute-done.2.came, f32[24,512]{1,0:T(8,128)S(1)} %collective-permute-done.3.near, f32[4,3,8,128]{3,2,1,0:T(8,128)S(1)} %shard_map.49.fixes), custom_call_target="tpu_custom_call" | custom-call | tf_op jit(solution)/shard_map/pallas_call | solution.py:574
  28.4 0.2 collective-permute-start.5
  28.6 5.5 %shard_map.50.kept = f32[2,3,128,128]{3,2,1,0:T(8,128)S(1)} custom-call(s32[6]{0:T(128)S(1)} %pad_add_fusion.lists, f32[4,2,256,128]{3,2,1,0:T(8,128)S(1)} %get-tuple-element.9.state, f32[24,512]{1,0:T(8,128)S(1)} %collective-permute-done.2.came, f32[24,512]{1,0:T(8,128)S(1)} %collective-permute-done.3.near, f32[4,3,8,128]{3,2,1,0:T(8,128)S(1)} %shard_map.49.fixes), custom_call_target="tpu_custom_call" | custom-call | tf_op jit(solution)/shard_map/pallas_call | solution.py:578
  34.1 0.0 collective-permute-done.4.inner
  34.1 4.9 %collective-permute-done.5.outer = f32[2,3,56,128]{3,2,1,0:T(8,128)S(1)} collective-permute-done((f32[2,3,56,128]{3,2,1,0:T(8,128)S(1)}, f32[2,3,56,128]{3,2,1,0:T(8,128)S(1)}, u32[]{:S(2)}, u32[]{:S(2)}) %collective-permute-start.5) | collective-permute-done | bytes 172064 | tf_op jit(solution)/shard_map/ppermute | solution.py:522
  39.0 1.6 %shard_map.53 = f32[3,3,128,128]{3,2,1,0:T(8,128)} custom-call(s32[6]{0:T(128)S(1)} %pad_add_fusion.lists, f32[2,3,128,128]{3,2,1,0:T(8,128)S(1)} %shard_map.50.kept, f32[2,3,80,128]{3,2,1,0:T(8,128)S(1)} %collective-permute-done.4.inner, f32[2,3,56,128]{3,2,1,0:T(8,128)S(1)} %collective-permute-done.5.outer), custom_call_target="tpu_custom_call" | custom-call | tf_op jit(solution)/shard_map/pallas_call | solution.py:584
  (1 shorter events, 0.0 us)
Async XLA Ops:
  0.0 0.7 %copy-start.3 = (s32[1,1,3]{2,1,0:T(1,128)S(1)}, s32[1,1,3]{2,1,0:T(1,128)}, u32[]{:S(2)}) copy-start(s32[1,1,3]{2,1,0:T(1,128)} %param.7) | copy-start | bytes 40
  0.7 7.5 %collective-permute-start = (s32[3]{0:T(128)S(1)}, s32[3]{0:T(128)S(1)}, u32[]{:S(2)}, u32[]{:S(2)}) collective-permute-start(s32[3]{0:T(128)S(1)} %bitcast.2), channel_id=1, source_target_pairs={{8,0},{10,2},{12,4},{14,6},{0,8},{2,10},{4,12},{6,14},{9,1},{11,3}... | collective-permute-start | bytes 44 | tf_op jit(solution)/shard_map/ppermute | solution.py:522
  4.7 1.0 %copy-start = (f32[2,256,256]{2,1,0:T(8,128)S(1)}, f32[2,256,256]{2,1,0:T(8,128)}, u32[]{:S(2)}) copy-start(f32[2,256,256]{2,1,0:T(8,128)} %velocity.1) | copy-start | bytes 1572868
  5.8 0.9 %copy-start.1 = (f32[256,256]{1,0:T(8,128)S(1)}, f32[256,256]{1,0:T(8,128)}, u32[]{:S(2)}) copy-start(f32[256,256]{1,0:T(8,128)} %depth.1) | copy-start | bytes 786436
  6.7 0.9 %copy-start.2 = (f32[256,256]{1,0:T(8,128)S(1)}, f32[256,256]{1,0:T(8,128)}, u32[]{:S(2)}) copy-start(f32[256,256]{1,0:T(8,128)} %bed.1) | copy-start | bytes 786436
  8.8 1.3 %collective-permute-start.1 = (f32[48,256]{1,0:T(8,128)S(1)}, f32[48,256]{1,0:T(8,128)S(1)}, u32[]{:S(2)}, u32[]{:S(2)}) collective-permute-start(f32[48,256]{1,0:T(8,128)S(1)} %get-tuple-element.12), channel_id=1, source_target_pairs={{0,1},{1,0},{2,3},{3,2},{4,5},{5,4},{6,7},{7,6},{8,9},{9,8},{10,11... | collective-permute-start | bytes 147464 | tf_op jit(solution)/shard_map/ppermute | solution.py:526
  10.1 9.5 %collective-permute-start.2 = (f32[24,512]{1,0:T(8,128)S(1)}, f32[24,512]{1,0:T(8,128)S(1)}, u32[]{:S(2)}, u32[]{:S(2)}) collective-permute-start(f32[24,512]{1,0:T(8,128)S(1)} %shard_map.48), channel_id=1, source_target_pairs={{2,1},{4,3},{6,5},{8,7},{10,9},{12,11},{14,13},{1,2},{3,4},{5,6},{... | collective-permute-start | bytes 147464 | tf_op jit(solution)/shard_map/ppermute | solution.py:557
  14.5 19.6 %collective-permute-start.4 = (f32[2,3,80,128]{3,2,1,0:T(8,128)S(1)}, f32[2,3,80,128]{3,2,1,0:T(8,128)S(1)}, u32[]{:S(2)}, u32[]{:S(2)}) collective-permute-start(f32[2,3,80,128]{3,2,1,0:T(8,128)S(1)} %shard_map.51), channel_id=1, source_target_pairs={{8,0},{10,2},{12,4},{14,6},{0,8},{2,10},{4,12},{6,14},{9,1},{11,3}... | collective-permute-start | bytes 737288 | tf_op jit(solution)/shard_map/ppermute | solution.py:522
  19.5 1.2 %collective-permute-start.3 = (f32[24,512]{1,0:T(8,128)S(1)}, f32[24,512]{1,0:T(8,128)S(1)}, u32[]{:S(2)}, u32[]{:S(2)}) collective-permute-start(f32[24,512]{1,0:T(8,128)S(1)} %collective-permute-done.2.came), channel_id=1, source_target_pairs={{0,1},{1,0},{2,3},{3,2},{4,5},{5,4},{6,7},{7,6},{8,9},{9,8},{10,11... | collective-permute-start | bytes 147464 | tf_op jit(solution)/shard_map/ppermute | solution.py:526
  28.4 10.6 %collective-permute-start.5 = (f32[2,3,56,128]{3,2,1,0:T(8,128)S(1)}, f32[2,3,56,128]{3,2,1,0:T(8,128)S(1)}, u32[]{:S(2)}, u32[]{:S(2)}) collective-permute-start(f32[2,3,56,128]{3,2,1,0:T(8,128)S(1)} %shard_map.52), channel_id=1, source_target_pairs={{8,0},{10,2},{12,4},{14,6},{0,8},{2,10},{4,12},{6,14},{9,1},{11,3}... | collective-permute-start | bytes 516104 | tf_op jit(solution)/shard_map/ppermute | solution.py:522

commit v4 on v3

--- a/solution.py
+++ b/solution.py
@@ -41,14 +41,15 @@
     return jax.ShapeDtypeStruct(shape, jnp.float32)
 
 
-def call(kernel, ins, outs, scratch=(), room=20 * 2**20):
+def call(kernel, ins, outs, scratch=(), out_specs=None, aliases=None):
     return pl.pallas_call(
         kernel,
         in_specs=list(ins),
-        out_specs=tuple(VMEM for _ in outs),
+        out_specs=out_specs or tuple(SMEM if o.dtype == jnp.int32 else VMEM for o in outs),
+        input_output_aliases=aliases or {},
         out_shape=tuple(outs),
         scratch_shapes=list(scratch),
-        compiler_params=pltpu.CompilerParams(vmem_limit_bytes=room),
+        compiler_params=pltpu.CompilerParams(vmem_limit_bytes=20 * 2**20),
     )
 
 
@@ -155,7 +156,7 @@
                 dst[f, w, rows, :] = src[f, w, rows, :] + TIME_STEP * (g - o)
 
 
-def load_kernel(depth, velocity, bed, state, turned, water, speed, ground, sems):
+def load_kernel(listed, depth, velocity, bed, state, turned, again, water, speed, ground, sems):
     copies = [
         pltpu.make_async_copy(depth, water, sems.at[0]),
         pltpu.make_async_copy(velocity, speed, sems.at[1]),
@@ -163,6 +164,8 @@
     ]
     for copy in copies:
         copy.start()
+    for k in range(SLOTS):
+        again[k] = listed[k]
     for copy in copies:
         copy.wait()
     for w in range(CT):
@@ -390,7 +393,7 @@
             out[k, f, OUTER : OUTER + 8, :] = fixes[tile[k], f]
 
 
-def keep_kernel(lists, state, came, near, fixes, out, start, middle, end, board):
+def keep_kernel(lists, state, came, near, fixes, packed, out, start, middle, end, board, sems):
     lists = Lists(lists)
     used, tile = lists.kept()
 
@@ -411,6 +414,21 @@
                 board,
                 store,
             )
+
+    out[MOVED] = jnp.zeros((3, TILE, TILE), jnp.float32)
+    copies = []
+    rank = jnp.int32(0)
+    for s in range(SLOTS):
+        entry = lists.listed[s]
+        own, _ = lists.inside(entry)
+        place = jnp.where(own, jnp.minimum(rank, MOVED - 1), MOVED)
+        rank = rank + own.astype(jnp.int32)
+        copy = pltpu.make_async_copy(out.at[place], packed.at[s], sems.at[s])
+        copies.append((own | (entry < 0), copy))
+    for due, copy in copies:
+        pl.when(due)(copy.start)
+    for due, copy in copies:
+        pl.when(due)(copy.wait)
 
 
 def seam_kernel(lists, turned, other, came, near, fixes, start, middle, end, one, two, side, board):
@@ -476,27 +494,26 @@
                 fixes[t, f, place : place + 4, :] = jnp.where(lane >= TILE - REACH, high, value)
 
 
-def pack_kernel(lists, kept, inner, outer, packed, board):
+def pack_kernel(lists, inner, outer, before, packed, staged, board, sems):
+    del before
     lists = Lists(lists)
     board[...] = jnp.zeros_like(board)
-    far = jnp.int32(0)
-    near = jnp.int32(0)
+    rank = jnp.int32(0)
+    copies = []
     for s in range(SLOTS):
         entry = lists.listed[s]
         own, _ = lists.inside(entry)
         foreign = (entry >= 0) & jnp.logical_not(own)
         top = lax.rem(lax.div(jnp.maximum(entry, 0), lists.span), RT) == 0
-        here = jnp.minimum(near, MOVED - 1)
-        there = jnp.minimum(far, MOVED - 1)
-        near = near + own.astype(jnp.int32)
-        far = far + foreign.astype(jnp.int32)
-
-        @pl.when(own)
-        def _(s=s, here=here):
-            packed[s] = kept[here]
+        there = jnp.minimum(rank, MOVED - 1)
+        rank = rank + foreign.astype(jnp.int32)
+        parts = [
+            pltpu.make_async_copy(staged.at[s, f], packed.at[s, f], sems.at[s, f]) for f in range(3)
+        ]
+        copies.append((foreign, parts))
 
         @pl.when(foreign)
-        def _(s=s, there=there, top=top):
+        def _(s=s, there=there, top=top, parts=parts):
             def cell(f, b):
                 high = jnp.where(top, b - OUTER, b)
                 low = jnp.where(top, b, b - INNER)
@@ -508,13 +525,18 @@
                 )
 
             def store(f, b, value):
-                packed[s, f, b : b + 8, :] = value
+                staged[s, f, b : b + 8, :] = value
+                if b == TILE - 8:
+                    parts[f].start()
 
             overlay(cell, lambda f: outer[there, f, OUTER : OUTER + 8, :], board, store)
 
-        @pl.when(entry < 0)
-        def _(s=s):
-            packed[s] = jnp.zeros((3, TILE, TILE), jnp.float32)
+    for foreign, parts in copies:
+
+        @pl.when(foreign)
+        def _(parts=parts):
+            for part in parts:
+                part.wait()
 
 
 def passed_along(block, distance):
@@ -524,6 +546,10 @@
 
 def swapped(block):
     return lax.ppermute(block, "cols", [(0, 1), (1, 0)])
+
+
+def in_hbm(block):
+    return pltpu.with_memory_space_constraint(block, pltpu.HBM)
 
 
 def scratch(*shape):
@@ -534,19 +560,23 @@
     count = lax.axis_size("rows")
     half = count // 2
     listed = slots[0, 0]
-    partner = passed_along(listed, half)
-    state, turned = call(
+    partner = passed_along(slots, half)[0, 0]
+    state, turned, again = call(
         load_kernel,
-        [HBM] * 3,
-        [f32(4, CT, ROWS, TILE), f32(4, 32, ROWS)],
+        [SMEM] + [HBM] * 3,
+        [
+            f32(4, CT, ROWS, TILE),
+            f32(4, 32, ROWS),
+            jax.ShapeDtypeStruct((SLOTS,), jnp.int32),
+        ],
         [
             scratch(ROWS, COLS),
             scratch(2, ROWS, COLS),
             scratch(ROWS, COLS),
             pltpu.SemaphoreType.DMA((3,)),
         ],
-    )(depth, velocity, bed)
-    lists = jnp.concatenate([listed, partner])
+    )(*[in_hbm(v) for v in (listed, depth, velocity, bed)])
+    lists = jnp.concatenate([again, partner])
     own, beside = call(edge_kernel, [SMEM, VMEM, VMEM], [f32(24, COLS), f32(48, COLS)])(
         lists, state, turned
     )
@@ -575,15 +605,29 @@
         outer_kernel, [SMEM] + [VMEM] * 4, [f32(MOVED, 3, OUTER + 8, TILE)], gathered + pair
     )(lists, state, came, near, fixes)
     far_outer = passed_along(outer, half)
-    (kept,) = call(
+    place = f32(SLOTS, 3, TILE, TILE)
+    (packed,) = call(
         keep_kernel,
         [SMEM] + [VMEM] * 4,
-        [f32(MOVED, 3, TILE, TILE)],
-        gathered + pair + [scratch(TILE, TILE)],
+        [place],
+        [scratch(MOVED + 1, 3, TILE, TILE)]
+        + gathered
+        + pair
+        + [scratch(TILE, TILE), pltpu.SemaphoreType.DMA((SLOTS,))],
+        (HBM,),
     )(lists, state, came, near, fixes)
     (packed,) = call(
-        pack_kernel, [SMEM] + [VMEM] * 3, [f32(SLOTS, 3, TILE, TILE)], [scratch(TILE, TILE)]
-    )(lists, kept, far_inner, far_outer)
+        pack_kernel,
+        [SMEM] + [VMEM] * 2 + [HBM],
+        [place],
+        [
+            scratch(SLOTS, 3, TILE, TILE),
+            scratch(TILE, TILE),
+            pltpu.SemaphoreType.DMA((SLOTS, 3)),
+        ],
+        (HBM,),
+        {3: 0},
+    )(lists, far_inner, far_outer, packed)
     return packed[None, None]
 
 

time: 40.9 us -> 39.6 us (0.968)
  local copies, waits for them, and re-layouts: 3.59 us -> 0 us
  Pallas kernels: 19.5 us -> 22.2 us
    unnamed x8 -> x0, local copies, waits for them, and re-layouts: 3.59 us -> none
    pallas_call x3, Pallas kernels: 7.56 us -> 10.3 us  [the longest x1 6.26 us: shards(): call(keep_kernel, [SMEM] + [VMEM] * 4, [place], [scratch(MOVED + 1, 3, TI...]
  transfers between devices with their start and end apart: 6 -> 6, of which waited for: 3 -> 3; matrix products, arithmetic and copies ran while one was open for 0% -> 0% of each run, Pallas kernels for 42% -> 51%
where the time goes in v4:
time: 39.6 us; the launch traced here: 39.5 us
  Pallas kernels  22.2 us (56%)
  starting transfers between devices  10.1 us (26%)
  waiting for transfers between devices  7.04 us (18%)
    ppermute x3, starting transfers between devices, passed_along(): lax.ppermute(block, 'rows', [((i - distance) % count, i) for i in range(c...  9.35 us
    pallas_call x1, Pallas kernels, shards(): call(keep_kernel, [SMEM] + [VMEM] * 4, [place], [scratch(MOVED + 1, 3, TI...  6.26 us
    ppermute x3, waiting for transfers between devices, passed_along(): lax.ppermute(block, 'rows', [((i - distance) % count, i) for i in range(c...  4.59 us
    pallas_call x1, Pallas kernels, shards(): call(seam_kernel, [SMEM] + [VMEM] * 4, [f32(RT * CT, 3, 8, TILE)], [scrat...  4.26 us
    pallas_call x1, Pallas kernels, shards(): call(inner_kernel, [SMEM, VMEM], [f32(MOVED, 3, INNER, TILE)], gathered +...  3.71 us
    pallas_call x1, Pallas kernels, shards(): call(outer_kernel, [SMEM] + [VMEM] * 4, [f32(MOVED, 3, OUTER + 8, TILE)],...  3.34 us
    pallas_call x1, Pallas kernels, shards(): call(load_kernel, [SMEM] + [HBM] * 3, [f32(4, CT, ROWS, TILE), f32(4, 32,...  2.5 us
    ppermute x2, waiting for transfers between devices, swapped(): return lax.ppermute(block, 'cols', [(0, 1), (1, 0)])  2.45 us
  transfers between devices with their start and end apart: 6, of which 3 were waited for; matrix products, arithmetic and copies ran while one was open for 0% of the time, Pallas kernels for 51%

profile of v4, /device:TPU:0, one launch (start us, length us, event | category | flops | bytes accessed | tf_op | source)
XLA Modules:
  0.0 39.5 jit_solution(6500080255698949944)
XLA Ops:
  0.0 4.1 %collective-permute-start = (s32[1,1,3]{2,1,0:T(1,128)}, s32[1,1,3]{2,1,0:T(1,128)S(1)}, u32[]{:S(2)}, u32[]{:S(2)}) collective-permute-start(s32[1,1,3]{2,1,0:T(1,128)} %param.7), channel_id=1, source_target_pairs={{8,0},{10,2},{12,4},{14,6},{0,8},{2,10},{4,12},{6,14},{9,1},{11,3}... | collective-permute-start | bytes 44 | tf_op jit(solution)/shard_map/ppermute | solution.py:544
  4.1 2.5 %shard_map.46 = (f32[4,2,256,128]{3,2,1,0:T(8,128)S(1)}, f32[4,32,256]{2,1,0:T(8,128)S(1)}, s32[3]{0:T(128)S(1)}) custom-call(s32[3]{0:T(128)} %bitcast.3, f32[256,256]{1,0:T(8,128)} %depth.1, f32[2,256,256]{2,1,0:T(8,128)} %velocity.1, f32[256,256]{1,0:T(8,128)} %bed.1), custom_call_target="tpu_custom_call" | custom-call | tf_op jit(solution)/shard_map/pallas_call | solution.py:564
  6.6 0.0 collective-permute-done
  6.6 0.1 pad_add_fusion.lists
  6.7 0.6 %shard_map.48 = (f32[24,256]{1,0:T(8,128)S(1)}, f32[48,256]{1,0:T(8,128)S(1)}) custom-call(s32[6]{0:T(128)S(1)} %pad_add_fusion.lists, f32[4,2,256,128]{3,2,1,0:T(8,128)S(1)} %get-tuple-element.11.state, f32[4,32,256]{2,1,0:T(8,128)S(1)} %get-tuple-element.12.turned), custom_call_target="tpu_custom_call" | custom-call | tf_op jit(solution)/shard_map/pallas_call | solution.py:580
  7.2 0.1 collective-permute-start.2
  7.3 1.2 %collective-permute-done.2.other = f32[48,256]{1,0:T(8,128)S(1)} collective-permute-done((f32[48,256]{1,0:T(8,128)S(1)}, f32[48,256]{1,0:T(8,128)S(1)}, u32[]{:S(2)}, u32[]{:S(2)}) %collective-permute-start.2) | collective-permute-done | bytes 49184 | tf_op jit(solution)/shard_map/ppermute | solution.py:548
  8.5 0.7 %collective-permute-start.3 = (f32[24,512]{1,0:T(8,128)S(1)}, f32[24,512]{1,0:T(8,128)S(1)}, u32[]{:S(2)}, u32[]{:S(2)}) collective-permute-start(f32[24,512]{1,0:T(8,128)S(1)} %shard_map.49), channel_id=1, source_target_pairs={{2,1},{4,3},{6,5},{8,7},{10,9},{12,11},{14,13},{1,2},{3,4},{5,6},{... | collective-permute-start | bytes 147464 | tf_op jit(solution)/shard_map/ppermute | solution.py:587
  9.2 3.7 %shard_map.47 = f32[2,3,80,128]{3,2,1,0:T(8,128)S(1)} custom-call(s32[6]{0:T(128)S(1)} %pad_add_fusion.lists, f32[4,2,256,128]{3,2,1,0:T(8,128)S(1)} %get-tuple-element.11.state), custom_call_target="tpu_custom_call" | custom-call | tf_op jit(solution)/shard_map/pallas_call | solution.py:590
  12.9 5.1 %collective-permute-start.1 = (f32[2,3,80,128]{3,2,1,0:T(8,128)S(1)}, f32[2,3,80,128]{3,2,1,0:T(8,128)S(1)}, u32[]{:S(2)}, u32[]{:S(2)}) collective-permute-start(f32[2,3,80,128]{3,2,1,0:T(8,128)S(1)} %shard_map.47), channel_id=1, source_target_pairs={{8,0},{10,2},{12,4},{14,6},{0,8},{2,10},{4,12},{6,14},{9,1},{11,3}... | collective-permute-start | bytes 737288 | tf_op jit(solution)/shard_map/ppermute | solution.py:544
  18.0 0.0 collective-permute-done.3.came
  18.0 0.0 collective-permute-start.4
  18.0 1.2 %collective-permute-done.4.near = f32[24,512]{1,0:T(8,128)S(1)} collective-permute-done((f32[24,512]{1,0:T(8,128)S(1)}, f32[24,512]{1,0:T(8,128)S(1)}, u32[]{:S(2)}, u32[]{:S(2)}) %collective-permute-start.4) | collective-permute-done | bytes 49184 | tf_op jit(solution)/shard_map/ppermute | solution.py:548
  19.2 4.3 %shard_map.50.fixes = f32[4,3,8,128]{3,2,1,0:T(8,128)S(1)} custom-call(s32[6]{0:T(128)S(1)} %pad_add_fusion.lists, f32[4,32,256]{2,1,0:T(8,128)S(1)} %get-tuple-element.12.turned, f32[48,256]{1,0:T(8,128)S(1)} %collective-permute-done.2.other, f32[24,512]{1,0:T(8,128)S(1)} %collective-permute-done.3.came, f32[24,512]{1,0:T(8,128)S(1)} %collective-permute-done.4.near), custom_call_target="tpu_custom_call" | custom-call | tf_op jit(solution)/shard_map/pallas_call | solution.py:595
  23.5 3.3 %shard_map.51 = f32[2,3,56,128]{3,2,1,0:T(8,128)S(1)} custom-call(s32[6]{0:T(128)S(1)} %pad_add_fusion.lists, f32[4,2,256,128]{3,2,1,0:T(8,128)S(1)} %get-tuple-element.11.state, f32[24,512]{1,0:T(8,128)S(1)} %collective-permute-done.3.came, f32[24,512]{1,0:T(8,128)S(1)} %collective-permute-done.4.near, f32[4,3,8,128]{3,2,1,0:T(8,128)S(1)} %shard_map.50.fixes), custom_call_target="tpu_custom_call" | custom-call | tf_op jit(solution)/shard_map/pallas_call | solution.py:604
  26.8 0.2 collective-permute-start.5
  27.1 6.3 %shard_map.52.before = f32[3,3,128,128]{3,2,1,0:T(8,128)} custom-call(s32[6]{0:T(128)S(1)} %pad_add_fusion.lists, f32[4,2,256,128]{3,2,1,0:T(8,128)S(1)} %get-tuple-element.11.state, f32[24,512]{1,0:T(8,128)S(1)} %collective-permute-done.3.came, f32[24,512]{1,0:T(8,128)S(1)} %collective-permute-done.4.near, f32[4,3,8,128]{3,2,1,0:T(8,128)S(1)} %shard_map.50.fixes), custom_call_target="tpu_custom_call" | custom-call | tf_op jit(solution)/shard_map/pallas_call | solution.py:609
  33.3 0.0 collective-permute-done.1.inner
  33.4 4.6 %collective-permute-done.5.outer = f32[2,3,56,128]{3,2,1,0:T(8,128)S(1)} collective-permute-done((f32[2,3,56,128]{3,2,1,0:T(8,128)S(1)}, f32[2,3,56,128]{3,2,1,0:T(8,128)S(1)}, u32[]{:S(2)}, u32[]{:S(2)}) %collective-permute-start.5) | collective-permute-done | bytes 172064 | tf_op jit(solution)/shard_map/ppermute | solution.py:544
  37.9 1.5 %shard_map.53 = f32[3,3,128,128]{3,2,1,0:T(8,128)} custom-call(s32[6]{0:T(128)S(1)} %pad_add_fusion.lists, f32[2,3,80,128]{3,2,1,0:T(8,128)S(1)} %collective-permute-done.1.inner, f32[2,3,56,128]{3,2,1,0:T(8,128)S(1)} %collective-permute-done.5.outer, f32[3,3,128,128]{3,2,1,0:T(8,128)} %shard_map.52.before), custom_call_target="tpu_custom_call", output_to_operand_aliasing={{}: (3, {})} | custom-call | tf_op jit(solution)/shard_map/pallas_call | solution.py:619
  (1 shorter events, 0.0 us)
Async XLA Ops:
  0.0 6.6 %collective-permute-start = (s32[1,1,3]{2,1,0:T(1,128)}, s32[1,1,3]{2,1,0:T(1,128)S(1)}, u32[]{:S(2)}, u32[]{:S(2)}) collective-permute-start(s32[1,1,3]{2,1,0:T(1,128)} %param.7), channel_id=1, source_target_pairs={{8,0},{10,2},{12,4},{14,6},{0,8},{2,10},{4,12},{6,14},{9,1},{11,3}... | collective-permute-start | bytes 44 | tf_op jit(solution)/shard_map/ppermute | solution.py:544
  7.2 1.3 %collective-permute-start.2 = (f32[48,256]{1,0:T(8,128)S(1)}, f32[48,256]{1,0:T(8,128)S(1)}, u32[]{:S(2)}, u32[]{:S(2)}) collective-permute-start(f32[48,256]{1,0:T(8,128)S(1)} %get-tuple-element.14), channel_id=1, source_target_pairs={{0,1},{1,0},{2,3},{3,2},{4,5},{5,4},{6,7},{7,6},{8,9},{9,8},{10,11... | collective-permute-start | bytes 147464 | tf_op jit(solution)/shard_map/ppermute | solution.py:548
  8.5 9.5 %collective-permute-start.3 = (f32[24,512]{1,0:T(8,128)S(1)}, f32[24,512]{1,0:T(8,128)S(1)}, u32[]{:S(2)}, u32[]{:S(2)}) collective-permute-start(f32[24,512]{1,0:T(8,128)S(1)} %shard_map.49), channel_id=1, source_target_pairs={{2,1},{4,3},{6,5},{8,7},{10,9},{12,11},{14,13},{1,2},{3,4},{5,6},{... | collective-permute-start | bytes 147464 | tf_op jit(solution)/shard_map/ppermute | solution.py:587
  12.9 20.4 %collective-permute-start.1 = (f32[2,3,80,128]{3,2,1,0:T(8,128)S(1)}, f32[2,3,80,128]{3,2,1,0:T(8,128)S(1)}, u32[]{:S(2)}, u32[]{:S(2)}) collective-permute-start(f32[2,3,80,128]{3,2,1,0:T(8,128)S(1)} %shard_map.47), channel_id=1, source_target_pairs={{8,0},{10,2},{12,4},{14,6},{0,8},{2,10},{4,12},{6,14},{9,1},{11,3}... | collective-permute-start | bytes 737288 | tf_op jit(solution)/shard_map/ppermute | solution.py:544
  18.0 1.2 %collective-permute-start.4 = (f32[24,512]{1,0:T(8,128)S(1)}, f32[24,512]{1,0:T(8,128)S(1)}, u32[]{:S(2)}, u32[]{:S(2)}) collective-permute-start(f32[24,512]{1,0:T(8,128)S(1)} %collective-permute-done.3.came), channel_id=1, source_target_pairs={{0,1},{1,0},{2,3},{3,2},{4,5},{5,4},{6,7},{7,6},{8,9},{9,8},{10,11... | collective-permute-start | bytes 147464 | tf_op jit(solution)/shard_map/ppermute | solution.py:548
  26.8 11.1 %collective-permute-start.5 = (f32[2,3,56,128]{3,2,1,0:T(8,128)S(1)}, f32[2,3,56,128]{3,2,1,0:T(8,128)S(1)}, u32[]{:S(2)}, u32[]{:S(2)}) collective-permute-start(f32[2,3,56,128]{3,2,1,0:T(8,128)S(1)} %shard_map.51), channel_id=1, source_target_pairs={{8,0},{10,2},{12,4},{14,6},{0,8},{2,10},{4,12},{6,14},{9,1},{11,3}... | collective-permute-start | bytes 516104 | tf_op jit(solution)/shard_map/ppermute | solution.py:544

commit v5 on v4

--- a/solution.py
+++ b/solution.py
@@ -20,10 +20,10 @@
 INNER = 80
 OUTER = TILE - INNER
 REACH = 4
-UNROLL_INNER = 3
-UNROLL_OUTER = 2
-UNROLL_FULL = 3
-UNROLL_SEAM = 1
+UNROLL_INNER = 6
+UNROLL_OUTER = 8
+UNROLL_FULL = 6
+UNROLL_SEAM = 5
 
 GRAVITY = 9.81
 TIME_STEP = 0.04
@@ -520,6 +520,8 @@
                 high = pl.multiple_of(jnp.clip(high, 0, INNER - 8), 8)
                 low = pl.multiple_of(jnp.clip(low, 0, OUTER - 8), 8)
                 within = jnp.where(top, b >= OUTER, b < INNER)
+                if OUTER <= b < INNER:
+                    return inner[there, f, pl.ds(high, 8), :]
                 return jnp.where(
                     within, inner[there, f, pl.ds(high, 8), :], outer[there, f, pl.ds(low, 8), :]
                 )

time: 39.6 us -> 38.2 us (0.965)
  Pallas kernels: 22.2 us -> 19.2 us
  waiting for transfers between devices: 7.04 us -> 8.6 us
    ppermute x3, waiting for transfers between devices: 4.59 us -> 6.15 us  [passed_along(): lax.ppermute(block, 'rows', [((i - distance) % count, i) for i in range(c...]
    pallas_call x1, Pallas kernels: 3.34 us -> 2.16 us  [shards(): call(outer_kernel, [SMEM] + [VMEM] * 4, [f32(MOVED, 3, OUTER + 8, TILE)],...]
    pallas_call x1, Pallas kernels: 6.26 us -> 5.11 us  [shards(): call(keep_kernel, [SMEM] + [VMEM] * 4, [place], [scratch(MOVED + 1, 3, TI...]
    pallas_call x1, Pallas kernels: 3.71 us -> 2.95 us  [shards(): call(inner_kernel, [SMEM, VMEM], [f32(MOVED, 3, INNER, TILE)], gathered +...]
  transfers between devices with their start and end apart: 6 -> 6, of which waited for: 3 -> 3; matrix products, arithmetic and copies ran while one was open for 0% -> 0% of each run, Pallas kernels for 51% -> 45%
where the time goes in v5:
time: 38.2 us; the launch traced here: 38 us
  Pallas kernels  19.2 us (50%)
  starting transfers between devices  10.1 us (26%)
  waiting for transfers between devices  8.6 us (23%)
    ppermute x3, starting transfers between devices, passed_along(): lax.ppermute(block, 'rows', [((i - distance) % count, i) for i in range(c...  9.33 us
    ppermute x3, waiting for transfers between devices, passed_along(): lax.ppermute(block, 'rows', [((i - distance) % count, i) for i in range(c...  6.15 us
    pallas_call x1, Pallas kernels, shards(): call(keep_kernel, [SMEM] + [VMEM] * 4, [place], [scratch(MOVED + 1, 3, TI...  5.11 us
    pallas_call x1, Pallas kernels, shards(): call(seam_kernel, [SMEM] + [VMEM] * 4, [f32(RT * CT, 3, 8, TILE)], [scrat...  4.36 us
    pallas_call x1, Pallas kernels, shards(): call(inner_kernel, [SMEM, VMEM], [f32(MOVED, 3, INNER, TILE)], gathered +...  2.95 us
    pallas_call x1, Pallas kernels, shards(): call(load_kernel, [SMEM] + [HBM] * 3, [f32(4, CT, ROWS, TILE), f32(4, 32,...  2.5 us
    ppermute x2, waiting for transfers between devices, swapped(): return lax.ppermute(block, 'cols', [(0, 1), (1, 0)])  2.45 us
    pallas_call x1, Pallas kernels, shards(): call(outer_kernel, [SMEM] + [VMEM] * 4, [f32(MOVED, 3, OUTER + 8, TILE)],...  2.16 us
  transfers between devices with their start and end apart: 6, of which 3 were waited for; matrix products, arithmetic and copies ran while one was open for 0% of the time, Pallas kernels for 45%

profile of v5, /device:TPU:0, one launch (start us, length us, event | category | flops | bytes accessed | tf_op | source)
XLA Modules:
  0.0 38.0 jit_solution(13916045300245601060)
XLA Ops:
  0.0 4.1 %collective-permute-start = (s32[1,1,3]{2,1,0:T(1,128)}, s32[1,1,3]{2,1,0:T(1,128)S(1)}, u32[]{:S(2)}, u32[]{:S(2)}) collective-permute-start(s32[1,1,3]{2,1,0:T(1,128)} %param.7), channel_id=1, source_target_pairs={{8,0},{10,2},{12,4},{14,6},{0,8},{2,10},{4,12},{6,14},{9,1},{11,3}... | collective-permute-start | bytes 44 | tf_op jit(solution)/shard_map/ppermute | solution.py:546
  4.1 2.5 %shard_map.46 = (f32[4,2,256,128]{3,2,1,0:T(8,128)S(1)}, f32[4,32,256]{2,1,0:T(8,128)S(1)}, s32[3]{0:T(128)S(1)}) custom-call(s32[3]{0:T(128)} %bitcast.3, f32[256,256]{1,0:T(8,128)} %depth.1, f32[2,256,256]{2,1,0:T(8,128)} %velocity.1, f32[256,256]{1,0:T(8,128)} %bed.1), custom_call_target="tpu_custom_call" | custom-call | tf_op jit(solution)/shard_map/pallas_call | solution.py:566
  6.6 0.0 collective-permute-done
  6.6 0.1 pad_add_fusion.lists
  6.7 0.6 %shard_map.48 = (f32[24,256]{1,0:T(8,128)S(1)}, f32[48,256]{1,0:T(8,128)S(1)}) custom-call(s32[6]{0:T(128)S(1)} %pad_add_fusion.lists, f32[4,2,256,128]{3,2,1,0:T(8,128)S(1)} %get-tuple-element.11.state, f32[4,32,256]{2,1,0:T(8,128)S(1)} %get-tuple-element.12.turned), custom_call_target="tpu_custom_call" | custom-call | tf_op jit(solution)/shard_map/pallas_call | solution.py:582
  7.2 0.1 collective-permute-start.2
  7.3 1.2 %collective-permute-done.2.other = f32[48,256]{1,0:T(8,128)S(1)} collective-permute-done((f32[48,256]{1,0:T(8,128)S(1)}, f32[48,256]{1,0:T(8,128)S(1)}, u32[]{:S(2)}, u32[]{:S(2)}) %collective-permute-start.2) | collective-permute-done | bytes 49184 | tf_op jit(solution)/shard_map/ppermute | solution.py:550
  8.5 0.7 %collective-permute-start.3 = (f32[24,512]{1,0:T(8,128)S(1)}, f32[24,512]{1,0:T(8,128)S(1)}, u32[]{:S(2)}, u32[]{:S(2)}) collective-permute-start(f32[24,512]{1,0:T(8,128)S(1)} %shard_map.49), channel_id=1, source_target_pairs={{2,1},{4,3},{6,5},{8,7},{10,9},{12,11},{14,13},{1,2},{3,4},{5,6},{... | collective-permute-start | bytes 147464 | tf_op jit(solution)/shard_map/ppermute | solution.py:589
  9.2 3.0 %shard_map.47 = f32[2,3,80,128]{3,2,1,0:T(8,128)S(1)} custom-call(s32[6]{0:T(128)S(1)} %pad_add_fusion.lists, f32[4,2,256,128]{3,2,1,0:T(8,128)S(1)} %get-tuple-element.11.state), custom_call_target="tpu_custom_call" | custom-call | tf_op jit(solution)/shard_map/pallas_call | solution.py:592
  12.2 5.1 %collective-permute-start.1 = (f32[2,3,80,128]{3,2,1,0:T(8,128)S(1)}, f32[2,3,80,128]{3,2,1,0:T(8,128)S(1)}, u32[]{:S(2)}, u32[]{:S(2)}) collective-permute-start(f32[2,3,80,128]{3,2,1,0:T(8,128)S(1)} %shard_map.47), channel_id=1, source_target_pairs={{8,0},{10,2},{12,4},{14,6},{0,8},{2,10},{4,12},{6,14},{9,1},{11,3}... | collective-permute-start | bytes 737288 | tf_op jit(solution)/shard_map/ppermute | solution.py:546
  17.2 0.0 collective-permute-done.3.came
  17.2 0.0 collective-permute-start.4
  17.2 1.2 %collective-permute-done.4.near = f32[24,512]{1,0:T(8,128)S(1)} collective-permute-done((f32[24,512]{1,0:T(8,128)S(1)}, f32[24,512]{1,0:T(8,128)S(1)}, u32[]{:S(2)}, u32[]{:S(2)}) %collective-permute-start.4) | collective-permute-done | bytes 49184 | tf_op jit(solution)/shard_map/ppermute | solution.py:550
  18.5 4.4 %shard_map.50.fixes = f32[4,3,8,128]{3,2,1,0:T(8,128)S(1)} custom-call(s32[6]{0:T(128)S(1)} %pad_add_fusion.lists, f32[4,32,256]{2,1,0:T(8,128)S(1)} %get-tuple-element.12.turned, f32[48,256]{1,0:T(8,128)S(1)} %collective-permute-done.2.other, f32[24,512]{1,0:T(8,128)S(1)} %collective-permute-done.3.came, f32[24,512]{1,0:T(8,128)S(1)} %collective-permute-done.4.near), custom_call_target="tpu_custom_call" | custom-call | tf_op jit(solution)/shard_map/pallas_call | solution.py:597
  22.8 2.2 %shard_map.51 = f32[2,3,56,128]{3,2,1,0:T(8,128)S(1)} custom-call(s32[6]{0:T(128)S(1)} %pad_add_fusion.lists, f32[4,2,256,128]{3,2,1,0:T(8,128)S(1)} %get-tuple-element.11.state, f32[24,512]{1,0:T(8,128)S(1)} %collective-permute-done.3.came, f32[24,512]{1,0:T(8,128)S(1)} %collective-permute-done.4.near, f32[4,3,8,128]{3,2,1,0:T(8,128)S(1)} %shard_map.50.fixes), custom_call_target="tpu_custom_call" | custom-call | tf_op jit(solution)/shard_map/pallas_call | solution.py:606
  25.0 0.2 collective-permute-start.5
  25.2 5.1 %shard_map.52.before = f32[3,3,128,128]{3,2,1,0:T(8,128)} custom-call(s32[6]{0:T(128)S(1)} %pad_add_fusion.lists, f32[4,2,256,128]{3,2,1,0:T(8,128)S(1)} %get-tuple-element.11.state, f32[24,512]{1,0:T(8,128)S(1)} %collective-permute-done.3.came, f32[24,512]{1,0:T(8,128)S(1)} %collective-permute-done.4.near, f32[4,3,8,128]{3,2,1,0:T(8,128)S(1)} %shard_map.50.fixes), custom_call_target="tpu_custom_call" | custom-call | tf_op jit(solution)/shard_map/pallas_call | solution.py:611
  30.3 0.0 collective-permute-done.1.inner
  30.3 6.1 %collective-permute-done.5.outer = f32[2,3,56,128]{3,2,1,0:T(8,128)S(1)} collective-permute-done((f32[2,3,56,128]{3,2,1,0:T(8,128)S(1)}, f32[2,3,56,128]{3,2,1,0:T(8,128)S(1)}, u32[]{:S(2)}, u32[]{:S(2)}) %collective-permute-start.5) | collective-permute-done | bytes 172064 | tf_op jit(solution)/shard_map/ppermute | solution.py:546
  36.5 1.5 %shard_map.53 = f32[3,3,128,128]{3,2,1,0:T(8,128)} custom-call(s32[6]{0:T(128)S(1)} %pad_add_fusion.lists, f32[2,3,80,128]{3,2,1,0:T(8,128)S(1)} %collective-permute-done.1.inner, f32[2,3,56,128]{3,2,1,0:T(8,128)S(1)} %collective-permute-done.5.outer, f32[3,3,128,128]{3,2,1,0:T(8,128)} %shard_map.52.before), custom_call_target="tpu_custom_call", output_to_operand_aliasing={{}: (3, {})} | custom-call | tf_op jit(solution)/shard_map/pallas_call | solution.py:621
  (1 shorter events, 0.0 us)
Async XLA Ops:
  0.0 6.6 %collective-permute-start = (s32[1,1,3]{2,1,0:T(1,128)}, s32[1,1,3]{2,1,0:T(1,128)S(1)}, u32[]{:S(2)}, u32[]{:S(2)}) collective-permute-start(s32[1,1,3]{2,1,0:T(1,128)} %param.7), channel_id=1, source_target_pairs={{8,0},{10,2},{12,4},{14,6},{0,8},{2,10},{4,12},{6,14},{9,1},{11,3}... | collective-permute-start | bytes 44 | tf_op jit(solution)/shard_map/ppermute | solution.py:546
  7.2 1.3 %collective-permute-start.2 = (f32[48,256]{1,0:T(8,128)S(1)}, f32[48,256]{1,0:T(8,128)S(1)}, u32[]{:S(2)}, u32[]{:S(2)}) collective-permute-start(f32[48,256]{1,0:T(8,128)S(1)} %get-tuple-element.14), channel_id=1, source_target_pairs={{0,1},{1,0},{2,3},{3,2},{4,5},{5,4},{6,7},{7,6},{8,9},{9,8},{10,11... | collective-permute-start | bytes 147464 | tf_op jit(solution)/shard_map/ppermute | solution.py:550
  8.5 8.7 %collective-permute-start.3 = (f32[24,512]{1,0:T(8,128)S(1)}, f32[24,512]{1,0:T(8,128)S(1)}, u32[]{:S(2)}, u32[]{:S(2)}) collective-permute-start(f32[24,512]{1,0:T(8,128)S(1)} %shard_map.49), channel_id=1, source_target_pairs={{2,1},{4,3},{6,5},{8,7},{10,9},{12,11},{14,13},{1,2},{3,4},{5,6},{... | collective-permute-start | bytes 147464 | tf_op jit(solution)/shard_map/ppermute | solution.py:589
  12.2 18.2 %collective-permute-start.1 = (f32[2,3,80,128]{3,2,1,0:T(8,128)S(1)}, f32[2,3,80,128]{3,2,1,0:T(8,128)S(1)}, u32[]{:S(2)}, u32[]{:S(2)}) collective-permute-start(f32[2,3,80,128]{3,2,1,0:T(8,128)S(1)} %shard_map.47), channel_id=1, source_target_pairs={{8,0},{10,2},{12,4},{14,6},{0,8},{2,10},{4,12},{6,14},{9,1},{11,3}... | collective-permute-start | bytes 737288 | tf_op jit(solution)/shard_map/ppermute | solution.py:546
  17.2 1.2 %collective-permute-start.4 = (f32[24,512]{1,0:T(8,128)S(1)}, f32[24,512]{1,0:T(8,128)S(1)}, u32[]{:S(2)}, u32[]{:S(2)}) collective-permute-start(f32[24,512]{1,0:T(8,128)S(1)} %collective-permute-done.3.came), channel_id=1, source_target_pairs={{0,1},{1,0},{2,3},{3,2},{4,5},{5,4},{6,7},{7,6},{8,9},{9,8},{10,11... | collective-permute-start | bytes 147464 | tf_op jit(solution)/shard_map/ppermute | solution.py:550
  25.0 11.5 %collective-permute-start.5 = (f32[2,3,56,128]{3,2,1,0:T(8,128)S(1)}, f32[2,3,56,128]{3,2,1,0:T(8,128)S(1)}, u32[]{:S(2)}, u32[]{:S(2)}) collective-permute-start(f32[2,3,56,128]{3,2,1,0:T(8,128)S(1)} %shard_map.51), channel_id=1, source_target_pairs={{8,0},{10,2},{12,4},{14,6},{0,8},{2,10},{4,12},{6,14},{9,1},{11,3}... | collective-permute-start | bytes 516104 | tf_op jit(solution)/shard_map/ppermute | solution.py:546
